TPU v7x, 32 devices: a whole 2x2x4 slice. The times are simulated.
32 devices in a mesh: group: 2 (over x), seq: 16 (over z, y, core).
Axes of the slice: x: 2, y: 2, z: 4, core: 2. Of those that a mesh axis runs over, the one named last changes fastest.
Arguments:
- prefix_key: bfloat16 [4096, 2048], P(('group', 'seq')), parts along dimension 0, may hold values from -6 to 6
- prefix_value: bfloat16 [4096, 2048], P(('group', 'seq')), parts along dimension 0, may hold values from -6 to 6
- prefix_kappa: bfloat16 [4096, 2048], P(('group', 'seq')), parts along dimension 0, may hold values from -6 to 6
- prefix_decay: bfloat16 [4096, 2048], P(('group', 'seq')), parts along dimension 0, as said below
- prefix_learn: bfloat16 [4096, 2048], P(('group', 'seq')), parts along dimension 0, may hold values from 0.0049743652 to 0.049804688
- answer_query: bfloat16 [32, 4, 8, 2048], P(('group', 'seq')), parts along dimension 0, may hold values from -6 to 6
- answer_key: bfloat16 [32, 4, 8, 2048], P(('group', 'seq')), parts along dimension 0, may hold values from -6 to 6
- answer_value: bfloat16 [32, 4, 8, 2048], P(('group', 'seq')), parts along dimension 0, may hold values from -6 to 6
- answer_kappa: bfloat16 [32, 4, 8, 2048], P(('group', 'seq')), parts along dimension 0, may hold values from -6 to 6
- answer_decay: bfloat16 [32, 4, 8, 2048], P(('group', 'seq')), parts along dimension 0, as said below
- answer_learn: bfloat16 [32, 4, 8, 2048], P(('group', 'seq')), parts along dimension 0, may hold values from 0.0049743652 to 0.049804688
- doc_lengths: int32 [8], P('group'), parts along dimension 0, may hold values from 1 to 8, as said below
- question_doc: int32 [32], P(('group', 'seq')), parts along dimension 0, may hold values from 0 to 3
- choice_tokens: int32 [32, 4, 8], P(('group', 'seq')), parts along dimension 0, may hold values from 0 to 65535
- choice_lengths: int32 [32, 4], P(('group', 'seq')), parts along dimension 0, may hold values from 1 to 8, 20 in all within a row
- head_weight: bfloat16 [2048, 65536], P(None, 'seq')
Outputs:
- scores: float32 [32, 4], P(('group', 'seq')), parts along dimension 0
There are 2 independent parts, one for each index of `group`. A program takes and returns all parts, laid end to end along the dimension named above; an argument that names none is the same for every part. Nothing has to cross between parts.
Inputs may be any that keep to these rules, and one draw needn't show every extreme that they name: `doc_lengths`: they sum to 16; the largest is exactly 8. `choice_lengths`: the lengths of one question's choices sum to 20, and the largest of them is exactly 8. `prefix_decay`: positive. `answer_decay`: positive.
All inputs are finite; a program needn't handle non-finite values.
Results may differ from a plain program's by a relative error of at most 0.0003.
The roundings to bfloat16 on the way count: a program that leaves them out, or rounds other values in their place, can miss the bound.
Values may be sent and summed in bfloat16 or wider, within the bound.
A program may use at most 128 MiB of HBM per device.

v0:
```python
import jax
import jax.numpy as jnp
from jax import lax
from jax.sharding import PartitionSpec as P

HSIZE = 64


def from_behind(block, axis, distance):
    devices = range(lax.axis_size(axis))
    route = [(i - distance, i) for i in devices if i - distance in devices]
    return lax.ppermute(block, axis, route)


def split_heads(tensor):
    return tensor.astype(jnp.float32).reshape(
        tensor.shape[:-1] + (tensor.shape[-1] // HSIZE, HSIZE)
    )


def transition(kappa, decay, learn):
    unit_kappa = kappa * lax.rsqrt(jnp.sum(kappa * kappa, -1, keepdims=True) + 1e-06)
    return (jnp.exp(-decay), unit_kappa, unit_kappa * learn)


def advance(memory, retain, unit_kappa, removal):
    projected = jnp.sum(memory * unit_kappa[..., None, :], -1, keepdims=True)
    return memory * retain[..., None, :] - projected * removal[..., None, :]


def group_norm(values):
    centre = values - jnp.mean(values, -1, keepdims=True)
    spread = jnp.mean(centre * centre, -1, keepdims=True)
    return centre * lax.rsqrt(spread + 1e-05)


def compose(first_part, second_part):
    return jnp.einsum("hvk,hkj->hvj", first_part, second_part, precision=lax.Precision.HIGHEST)


def local(
    prefix_key,
    prefix_value,
    prefix_kappa,
    prefix_decay,
    prefix_learn,
    answer_query,
    answer_key,
    answer_value,
    answer_kappa,
    answer_decay,
    answer_learn,
    doc_lengths,
    question_doc,
    choice_tokens,
    choice_lengths,
    head_weight,
):
    tok_rows, row_width = prefix_key.shape
    head_count = row_width // HSIZE
    shards = lax.axis_size("seq")
    my_index = lax.axis_index("seq")
    doc_ends = jnp.cumsum(doc_lengths)
    doc_starts = doc_ends - doc_lengths
    opened = jnp.any(doc_starts == my_index)
    identity = jnp.broadcast_to(jnp.eye(HSIZE, dtype=jnp.float32), (head_count, HSIZE, HSIZE))
    empty_state = jnp.zeros((head_count, HSIZE, HSIZE), jnp.float32)
    block_count = tok_rows // 16

    def blocked(tensor):
        return tensor.reshape(block_count, 16, row_width)

    def block_step(states, inputs):
        for position in range(16):
            key_now, value_now, kappa_now, decay_now, learn_now = [
                split_heads(tensor[position]) for tensor in inputs
            ]
            retain, unit_kappa, removal = transition(kappa_now, decay_now, learn_now)
            states = advance(states, retain, unit_kappa, removal)
            states = states.at[1].add(value_now[:, :, None] * key_now[:, None, :])
        return (states, None)

    states, _ = lax.scan(
        block_step,
        jnp.stack([identity, empty_state]),
        (
            blocked(prefix_key),
            blocked(prefix_value),
            blocked(prefix_kappa),
            blocked(prefix_decay),
            blocked(prefix_learn),
        ),
    )
    passage = jnp.where(opened, jnp.float32(0.0), states[0])
    update = states[1]
    answer_states = jnp.broadcast_to(identity, answer_query.shape[:2] + identity.shape)
    answer_states = jnp.stack([answer_states, jnp.zeros_like(answer_states)])
    per_token = []
    for step in range(answer_query.shape[2]):
        query_now = split_heads(answer_query[:, :, step])
        key_now = split_heads(answer_key[:, :, step])
        value_now = split_heads(answer_value[:, :, step])
        retain, unit_kappa, removal = transition(
            split_heads(answer_kappa[:, :, step]),
            split_heads(answer_decay[:, :, step]),
            split_heads(answer_learn[:, :, step]),
        )
        answer_states = advance(answer_states, retain, unit_kappa, removal)
        answer_states = answer_states.at[1].add(value_now[..., :, None] * key_now[..., None, :])
        per_token.append(jnp.sum(answer_states * query_now[..., None, :], -1))
    pulled = jnp.stack(per_token, 3)

    def relay_step(turn, carried):
        arrived = from_behind(carried[0], "seq", 1)
        return (compose(arrived, passage) + update, arrived)

    end_state, incoming = lax.fori_loop(0, shards - 1, relay_step, (update, empty_state))
    sendable = end_state.astype(jnp.bfloat16)
    doc_count = doc_lengths.shape[0]
    doc_match = question_doc[:, None] == jnp.arange(doc_count, dtype=jnp.int32)[None, :]
    source_dev = jnp.sum(jnp.where(doc_match, doc_ends[None, :] - 1, 0), 1)
    piece = lax.all_gather(sendable[None], "seq", axis=0, tiled=True)
    indices = jnp.arange(piece.shape[0], dtype=jnp.int32)
    chosen = (source_dev[:, None] == indices[None, :]).astype(jnp.bfloat16)
    start_state = jnp.einsum("qn,nhvk->qhvk", chosen, piece, preferred_element_type=jnp.float32)
    output = (
        jnp.einsum("qhvk,qcthk->qcthv", start_state, pulled[0], precision=lax.Precision.HIGHEST)
        + pulled[1]
    )
    hidden = group_norm(output).reshape(-1, row_width).astype(jnp.bfloat16)
    targets = choice_tokens.reshape(-1)
    local_rows = hidden.shape[0]
    vocab_dev = head_weight.shape[1]
    vocab_offset = my_index * vocab_dev
    part_rows = lax.all_gather(hidden, "seq", axis=0, tiled=True)
    part_ids = lax.all_gather(targets, "seq", axis=0, tiled=True)
    logits = jnp.dot(part_rows, head_weight, preferred_element_type=jnp.float32)
    peak_logit = jnp.max(logits, -1)
    exp_mass = jnp.sum(jnp.exp(logits - peak_logit[:, None]), -1)
    columns = jnp.arange(vocab_dev, dtype=jnp.int32) + vocab_offset
    picked = jnp.sum(jnp.where(columns[None, :] == part_ids[:, None], logits, jnp.float32(0.0)), -1)
    peak_all, mass_all, picked_all = tuple(
        (new_value for new_value in (peak_logit, exp_mass, picked))
    )
    peak_parts, mass_parts, picked_parts = (
        lax.all_to_all(
            peak_all.reshape(shards, local_rows), "seq", split_axis=0, concat_axis=0, tiled=True
        ),
        lax.all_to_all(
            mass_all.reshape(shards, local_rows), "seq", split_axis=0, concat_axis=0, tiled=True
        ),
        lax.all_to_all(
            picked_all.reshape(shards, local_rows), "seq", split_axis=0, concat_axis=0, tiled=True
        ),
    )
    overall_peak = jnp.max(peak_parts, 0)
    total = overall_peak + jnp.log(
        jnp.sum(mass_parts * jnp.exp(peak_parts - overall_peak[None, :]), 0)
    )
    logprob = (jnp.sum(picked_parts, 0) - total).reshape(choice_tokens.shape)
    inside = (
        jnp.arange(choice_tokens.shape[2], dtype=jnp.int32)[None, None, :]
        < choice_lengths[:, :, None]
    )
    return jnp.sum(jnp.where(inside, logprob, jnp.float32(0.0)), -1) / choice_lengths.astype(
        jnp.float32
    )


def solution(mesh):
    placed = (
        P(("group", "seq"), None),
        P(("group", "seq"), None),
        P(("group", "seq"), None),
        P(("group", "seq"), None),
        P(("group", "seq"), None),
        P(("group", "seq"), None, None, None),
        P(("group", "seq"), None, None, None),
        P(("group", "seq"), None, None, None),
        P(("group", "seq"), None, None, None),
        P(("group", "seq"), None, None, None),
        P(("group", "seq"), None, None, None),
        P("group"),
        P(("group", "seq")),
        P(("group", "seq"), None, None),
        P(("group", "seq"), None),
        P(None, "seq"),
    )
    return jax.shard_map(
        local, mesh=mesh, in_specs=placed, out_specs=P(("group", "seq"), None), check_vma=False
    )
```

profile of v0, /device:TPU:0, one launch (start us, length us, event | category | flops | bytes accessed | tf_op | source)
XLA Modules:
  0.0 1475.5 jit_solution(15536502433968630703)
XLA Ops:
  8.3 951.8 %while.46 = (s32[]{:T(128)}, f32[2,32,64,64]{3,2,1,0:T(8,128)}, bf16[8,16,2048]{2,1,0:T(8,128)(2,1)}, bf16[8,16,2048]{2,1,0:T(8,128)(2,1)}, bf16[8,16,2048]{2,1,...) while((s32[]{:T(128)}, f32[2,32,64,64]{3,2,1,0:T(8,128)}, ...), condition=%wide.region_59.60_spmd, body=%wide.region_26.59_spmd.sunk | while | flops 25427984 | bytes 146760688 | solution.py:83
  964.2 266.0 %while.47 = (s32[]{:T(128)}, f32[32,64,64]{2,1,0:T(8,128)}, f32[32,64,64]{2,1,0:T(8,128)S(1)}, f32[32,64,64]{2,1,0:T(8,128)S(1)}, s32[]{:T(128)}) while((s32[]{:T(128)}, f32[32,64,64]{2,1,0:T(8,128)}, f32[32,64,64]{2,1,0:T(8,128)S(1)}, f32[32,64,64]{2,1,0:T(8,128)S(1)}, s32[]{:T(128)}) %tuple.368), condition=%wide.region_62.63_spmd, body=%wide.region_61.62_spmd.sunk | while | flops 100794368 | bytes 4194405 | solution.py:117
  971.2 14.1 collective-permute-start
  989.9 13.9 collective-permute-start
  1008.4 13.9 collective-permute-start
  1026.9 13.9 collective-permute-start
  1045.4 13.9 collective-permute-start
  1063.9 13.9 collective-permute-start
  1082.3 13.9 collective-permute-start
  1100.8 13.9 collective-permute-start
  1119.3 13.9 collective-permute-start
  1137.8 13.9 collective-permute-start
  1156.3 13.9 collective-permute-start
  1174.8 13.9 collective-permute-start
  1193.2 13.9 collective-permute-start
  1211.7 13.9 collective-permute-start
  1264.7 5.8 multiply_subtract_fusion.21
  1290.5 6.0 multiply_subtract_fusion.19
  1341.7 8.9 fusion.210
  1355.9 37.8 %all-reduce.2 = s32[512]{0:T(512)S(1)} all-reduce(s32[512]{0:T(512)S(1)} %dynamic-update-slice.120), channel_id=1, replica_groups=mesh['group'=2,'seq'=16] {'seq'}, use_global_device_ids=true, to_apply=%add.2 | all-reduce | flops 512 | bytes 4096
  1393.7 28.6 %all-gather.4.cloned.1.call-done = bf16[512,2048]{1,0:T(8,128)(2,1)} async-done(((bf16[32,2048]{1,0:T(8,128)(2,1)}), bf16[512,2048]{1,0:T(8,128)(2,1)}) %all-gather.4.cloned.1.call-update) | async-done | bytes 2097168 | tf_op jit(solution)/shard_map/all_gather | solution.py:135
  1422.3 12.6 fusion.260
  1442.1 5.7 all-to-all-done
  1461.2 6.3 all-to-all-done.2
  (1885 shorter events, 1151.0 us)
Async XLA Ops:
  6.5 1335.2 %all-gather.6.cloned.1.call-start = ((), (), s32[]{:S(2)}) async-start(), calls=%async_computation.4 | async-start | bytes 8912896 | tf_op jit(solution)/shard_map/all_gather | solution.py:122
  8.3 951.8 %copy-start.30 = (s32[4]{0:T(128)S(1)}, s32[4]{0:T(128)}, u32[]{:S(2)}) copy-start(s32[4]{0:T(128)} %param.79) | copy-start | bytes 52
  964.2 4.8 collective-permute-start
  971.2 16.6 %collective-permute-start = (f32[32,64,64]{2,1,0:T(8,128)}, f32[32,64,64]{2,1,0:T(8,128)S(1)}, u32[]{:S(2)}, u32[]{:S(2)}) collective-permute-start(f32[32,64,64]{2,1,0:T(8,128)} %get-tuple-element.1037), channel_id=1, source_target_pairs={{0,1},{1,2},{2,3},{3,4},{4,5},{5,6},{6,7},{7,8},{8,9},{9,10},{10,1... | collective-permute-start | bytes 1572872 | tf_op jit(solution)/shard_map/while/body/eval_jaxpr/ppermute | solution.py:12
  989.9 16.3 %collective-permute-start = (f32[32,64,64]{2,1,0:T(8,128)}, f32[32,64,64]{2,1,0:T(8,128)S(1)}, u32[]{:S(2)}, u32[]{:S(2)}) collective-permute-start(f32[32,64,64]{2,1,0:T(8,128)} %get-tuple-element.1037), channel_id=1, source_target_pairs={{0,1},{1,2},{2,3},{3,4},{4,5},{5,6},{6,7},{7,8},{8,9},{9,10},{10,1... | collective-permute-start | bytes 1572872 | tf_op jit(solution)/shard_map/while/body/eval_jaxpr/ppermute | solution.py:12
  1008.4 16.3 %collective-permute-start = (f32[32,64,64]{2,1,0:T(8,128)}, f32[32,64,64]{2,1,0:T(8,128)S(1)}, u32[]{:S(2)}, u32[]{:S(2)}) collective-permute-start(f32[32,64,64]{2,1,0:T(8,128)} %get-tuple-element.1037), channel_id=1, source_target_pairs={{0,1},{1,2},{2,3},{3,4},{4,5},{5,6},{6,7},{7,8},{8,9},{9,10},{10,1... | collective-permute-start | bytes 1572872 | tf_op jit(solution)/shard_map/while/body/eval_jaxpr/ppermute | solution.py:12
  1026.9 16.3 %collective-permute-start = (f32[32,64,64]{2,1,0:T(8,128)}, f32[32,64,64]{2,1,0:T(8,128)S(1)}, u32[]{:S(2)}, u32[]{:S(2)}) collective-permute-start(f32[32,64,64]{2,1,0:T(8,128)} %get-tuple-element.1037), channel_id=1, source_target_pairs={{0,1},{1,2},{2,3},{3,4},{4,5},{5,6},{6,7},{7,8},{8,9},{9,10},{10,1... | collective-permute-start | bytes 1572872 | tf_op jit(solution)/shard_map/while/body/eval_jaxpr/ppermute | solution.py:12
  1045.4 16.3 %collective-permute-start = (f32[32,64,64]{2,1,0:T(8,128)}, f32[32,64,64]{2,1,0:T(8,128)S(1)}, u32[]{:S(2)}, u32[]{:S(2)}) collective-permute-start(f32[32,64,64]{2,1,0:T(8,128)} %get-tuple-element.1037), channel_id=1, source_target_pairs={{0,1},{1,2},{2,3},{3,4},{4,5},{5,6},{6,7},{7,8},{8,9},{9,10},{10,1... | collective-permute-start | bytes 1572872 | tf_op jit(solution)/shard_map/while/body/eval_jaxpr/ppermute | solution.py:12
  1063.9 16.3 %collective-permute-start = (f32[32,64,64]{2,1,0:T(8,128)}, f32[32,64,64]{2,1,0:T(8,128)S(1)}, u32[]{:S(2)}, u32[]{:S(2)}) collective-permute-start(f32[32,64,64]{2,1,0:T(8,128)} %get-tuple-element.1037), channel_id=1, source_target_pairs={{0,1},{1,2},{2,3},{3,4},{4,5},{5,6},{6,7},{7,8},{8,9},{9,10},{10,1... | collective-permute-start | bytes 1572872 | tf_op jit(solution)/shard_map/while/body/eval_jaxpr/ppermute | solution.py:12
  1082.3 16.3 %collective-permute-start = (f32[32,64,64]{2,1,0:T(8,128)}, f32[32,64,64]{2,1,0:T(8,128)S(1)}, u32[]{:S(2)}, u32[]{:S(2)}) collective-permute-start(f32[32,64,64]{2,1,0:T(8,128)} %get-tuple-element.1037), channel_id=1, source_target_pairs={{0,1},{1,2},{2,3},{3,4},{4,5},{5,6},{6,7},{7,8},{8,9},{9,10},{10,1... | collective-permute-start | bytes 1572872 | tf_op jit(solution)/shard_map/while/body/eval_jaxpr/ppermute | solution.py:12
  1100.8 16.3 %collective-permute-start = (f32[32,64,64]{2,1,0:T(8,128)}, f32[32,64,64]{2,1,0:T(8,128)S(1)}, u32[]{:S(2)}, u32[]{:S(2)}) collective-permute-start(f32[32,64,64]{2,1,0:T(8,128)} %get-tuple-element.1037), channel_id=1, source_target_pairs={{0,1},{1,2},{2,3},{3,4},{4,5},{5,6},{6,7},{7,8},{8,9},{9,10},{10,1... | collective-permute-start | bytes 1572872 | tf_op jit(solution)/shard_map/while/body/eval_jaxpr/ppermute | solution.py:12
  1119.3 16.3 %collective-permute-start = (f32[32,64,64]{2,1,0:T(8,128)}, f32[32,64,64]{2,1,0:T(8,128)S(1)}, u32[]{:S(2)}, u32[]{:S(2)}) collective-permute-start(f32[32,64,64]{2,1,0:T(8,128)} %get-tuple-element.1037), channel_id=1, source_target_pairs={{0,1},{1,2},{2,3},{3,4},{4,5},{5,6},{6,7},{7,8},{8,9},{9,10},{10,1... | collective-permute-start | bytes 1572872 | tf_op jit(solution)/shard_map/while/body/eval_jaxpr/ppermute | solution.py:12
  1137.8 16.3 %collective-permute-start = (f32[32,64,64]{2,1,0:T(8,128)}, f32[32,64,64]{2,1,0:T(8,128)S(1)}, u32[]{:S(2)}, u32[]{:S(2)}) collective-permute-start(f32[32,64,64]{2,1,0:T(8,128)} %get-tuple-element.1037), channel_id=1, source_target_pairs={{0,1},{1,2},{2,3},{3,4},{4,5},{5,6},{6,7},{7,8},{8,9},{9,10},{10,1... | collective-permute-start | bytes 1572872 | tf_op jit(solution)/shard_map/while/body/eval_jaxpr/ppermute | solution.py:12
  1156.3 16.3 %collective-permute-start = (f32[32,64,64]{2,1,0:T(8,128)}, f32[32,64,64]{2,1,0:T(8,128)S(1)}, u32[]{:S(2)}, u32[]{:S(2)}) collective-permute-start(f32[32,64,64]{2,1,0:T(8,128)} %get-tuple-element.1037), channel_id=1, source_target_pairs={{0,1},{1,2},{2,3},{3,4},{4,5},{5,6},{6,7},{7,8},{8,9},{9,10},{10,1... | collective-permute-start | bytes 1572872 | tf_op jit(solution)/shard_map/while/body/eval_jaxpr/ppermute | solution.py:12
  1174.8 16.3 %collective-permute-start = (f32[32,64,64]{2,1,0:T(8,128)}, f32[32,64,64]{2,1,0:T(8,128)S(1)}, u32[]{:S(2)}, u32[]{:S(2)}) collective-permute-start(f32[32,64,64]{2,1,0:T(8,128)} %get-tuple-element.1037), channel_id=1, source_target_pairs={{0,1},{1,2},{2,3},{3,4},{4,5},{5,6},{6,7},{7,8},{8,9},{9,10},{10,1... | collective-permute-start | bytes 1572872 | tf_op jit(solution)/shard_map/while/body/eval_jaxpr/ppermute | solution.py:12
  1193.2 16.3 %collective-permute-start = (f32[32,64,64]{2,1,0:T(8,128)}, f32[32,64,64]{2,1,0:T(8,128)S(1)}, u32[]{:S(2)}, u32[]{:S(2)}) collective-permute-start(f32[32,64,64]{2,1,0:T(8,128)} %get-tuple-element.1037), channel_id=1, source_target_pairs={{0,1},{1,2},{2,3},{3,4},{4,5},{5,6},{6,7},{7,8},{8,9},{9,10},{10,1... | collective-permute-start | bytes 1572872 | tf_op jit(solution)/shard_map/while/body/eval_jaxpr/ppermute | solution.py:12
  1211.7 16.3 %collective-permute-start = (f32[32,64,64]{2,1,0:T(8,128)}, f32[32,64,64]{2,1,0:T(8,128)S(1)}, u32[]{:S(2)}, u32[]{:S(2)}) collective-permute-start(f32[32,64,64]{2,1,0:T(8,128)} %get-tuple-element.1037), channel_id=1, source_target_pairs={{0,1},{1,2},{2,3},{3,4},{4,5},{5,6},{6,7},{7,8},{8,9},{9,10},{10,1... | collective-permute-start | bytes 1572872 | tf_op jit(solution)/shard_map/while/body/eval_jaxpr/ppermute | solution.py:12
  1230.2 5.8 copy-start.24
  1232.4 189.9 %all-gather.4.cloned.1.call-start = ((), (), s32[]{:S(2)}) async-start(), calls=%async_computation.3 | async-start | bytes 2228224 | tf_op jit(solution)/shard_map/all_gather | solution.py:135
  1233.3 5.7 copy-start.28
  1434.9 32.8 %copy-start.31 = (s32[1,4]{1,0:T(1,128)S(1)}, s32[1,4]{1,0:T(1,128)}, u32[]{:S(2)}) copy-start(s32[1,4]{1,0:T(1,128)} %param.82) | copy-start | bytes 52
  1438.0 9.9 all-to-all-start
  1447.9 9.9 all-to-all-start.1
  1457.7 9.8 all-to-all-start.2
  (127 other events, 376.5 us)
Sparse Core Ops, SparseCore 0:
  1232.5 101.3 all-gather.5
  1354.5 67.8 all-gather.3
where the time goes:
time: 1480 us
  other arithmetic  1010 us (68%)
  starting transfers between devices  208 us (14%)
  waiting for transfers between devices  82.5 us (6%)
  local copies, waits for them, and re-layouts  60.8 us (4%)
  matrix products  55.8 us (4%)
  blocking collectives  37.8 us (3%)
  between operations  15.7 us (1%)
    reduce_sum x136, other arithmetic, advance(): projected = jnp.sum(memory * unit_kappa[..., None, :], -1, keepdims=True)  324 us
    scatter-add x128, other arithmetic, block_step(): states = states.at[1].add(value_now[:, :, None] * key_now[:, None, :])  317 us
    sub x136, other arithmetic, advance(): return memory * retain[..., None, :] - projected * removal[..., None, :]  260 us
    ppermute x15, starting transfers between devices, from_behind(): return lax.ppermute(block, axis, route)  197 us
    convert_element_type x20, other arithmetic, split_heads(): tensor.astype(jnp.float32)  42.5 us
    convert_element_type x552, local copies, waits for them, and re-layouts, split_heads(): tensor.astype(jnp.float32)  39.9 us
    unnamed x1, blocking collectives  37.8 us
    ppermute x15, waiting for transfers between devices, from_behind(): return lax.ppermute(block, axis, route)  36.2 us
  transfers between devices with their start and end apart: 20, of which 19 were waited for; matrix products, arithmetic and copies ran while one was open for 7% of the time, Pallas kernels for 0%

commit v1 on v0

v1 whole, which is shorter than its diff:
```python
import functools

import jax
import jax.numpy as jnp
from jax import lax
from jax.experimental import pallas as pl
from jax.experimental.pallas import tpu as pltpu
from jax.sharding import PartitionSpec as P

HSIZE = 64
LANES = 128
WIDE = 256
CHUNK = 16
F32 = jnp.float32
BF16 = jnp.bfloat16


def split(x):
    high = x.astype(BF16)
    return high, (x - high.astype(F32)).astype(BF16)


def mm(a, b, dims):
    return lax.dot_general(a, b, (dims, ((), ())), preferred_element_type=F32)


NN = ((1,), (0,))
TN = ((0,), (0,))
NT = ((1,), (1,))


def dot3(a, b, dims=NN):
    ah, al = split(a)
    bh, bl = split(b)
    return mm(ah, bh, dims) + (mm(al, bh, dims) + mm(ah, bl, dims))


def block_mask(rows, cols):
    return (
        lax.broadcasted_iota(jnp.int32, (rows, cols), 0) // HSIZE
        == lax.broadcasted_iota(jnp.int32, (rows, cols), 1) // HSIZE
    )


def head_sum(x, ones):
    high, low = split(x)
    return mm(high, ones, NN) + mm(low, ones, NN)


def stack_heads(x):
    heads = x.shape[1] // HSIZE
    lane = lax.broadcasted_iota(jnp.int32, x.shape, 1) // HSIZE
    return jnp.concatenate([jnp.where(lane == h, x, jnp.zeros_like(x)) for h in range(heads)], 0)


def fold_heads(x):
    heads = x.shape[1] // HSIZE
    out = x[:HSIZE]
    for h in range(1, heads):
        out = out + x[h * HSIZE : (h + 1) * HSIZE]
    return out


def factors(kappa, decay, learn, ones):
    kappa = kappa.astype(F32)
    unit = kappa * lax.rsqrt(head_sum(kappa * kappa, ones) + 1e-06)
    return jnp.exp(-decay.astype(F32)), unit, unit * learn.astype(F32)


def prefix_group(key, value, kappa, decay, learn, ones, diag_block):
    rows, wide = key.shape
    chunks = rows // CHUNK
    retain, unit, removal = factors(kappa, decay, learn, ones)

    def halves(x):
        x = x.reshape(chunks, 2, 8, wide)
        return [x[:, 0], x[:, 1]]

    retain, unit, removal = halves(retain), halves(unit), halves(removal)
    sub = lax.broadcasted_iota(jnp.int32, (chunks, 8, wide), 1)

    def at(parts, step):
        return parts[step // 8][:, step % 8 : step % 8 + 1, :]

    def segments(x):
        return head_sum(x.reshape(chunks * 8, wide), ones).reshape(chunks, 8, wide)

    pushed = halves(key.astype(F32))
    for step in range(1, CHUNK):
        r, u, w = at(retain, step), at(unit, step), at(removal, step)
        for half in range(step // 8 + 1):
            if half * 8 >= step:
                continue
            x = pushed[half]
            new = x * r - segments(x * u) * w
            pushed[half] = new if step >= half * 8 + 8 else jnp.where(sub < step - half * 8, new, x)
    pulled = list(unit)
    for step in range(CHUNK - 2, -1, -1):
        r, u, w = at(retain, step), at(unit, step), at(removal, step)
        for half in range(2):
            if half * 8 + 7 <= step:
                continue
            x = pulled[half]
            new = x * r - segments(x * w) * u
            pulled[half] = new if step < half * 8 else jnp.where(sub > step - half * 8, new, x)
    tail = jnp.ones((chunks, 1, wide), F32)
    faded = [None] * CHUNK
    for step in range(CHUNK - 1, -1, -1):
        faded[step] = at(removal, step) * tail
        tail = tail * at(retain, step)

    def joined(parts):
        return jnp.concatenate([p.reshape(chunks, 1, 8, wide) for p in parts], 1).reshape(rows, wide)

    def spread(items):
        out = jnp.zeros((chunks, 8, wide), F32)
        for spot, item in enumerate(items):
            out = jnp.where(sub == spot, item, out)
        return out

    faded = joined([spread(faded[:8]), spread(faded[8:])])
    pulled = joined(pulled)
    pushed = joined(pushed)
    eye = lax.broadcasted_iota(jnp.int32, (wide, wide), 0) == lax.broadcasted_iota(
        jnp.int32, (wide, wide), 1
    )
    passage = None
    keys = None
    for c in range(chunks):
        part = slice(c * CHUNK, (c + 1) * CHUNK)
        low_rank = dot3(pulled[part], faded[part], TN)
        whole = jnp.where(eye, tail[c], 0.0) - jnp.where(diag_block, low_rank, 0.0)
        if c == 0:
            passage = fold_heads(whole)
            keys = pushed[part]
        else:
            moved = dot3(jnp.concatenate([passage, keys], 0), whole)
            passage = moved[:HSIZE]
            keys = jnp.concatenate([moved[HSIZE:], pushed[part]], 0)
    high, low = split(keys)
    outer = mm(value, high, TN) + mm(value, low, TN)
    return passage, fold_heads(jnp.where(diag_block, outer, 0.0))


def answer_group(query, key, value, kappa, decay, learn, ones):
    rows, wide = query.shape
    count = rows // 8
    retain, unit, removal = factors(kappa, decay, learn, ones)

    def tiled(x):
        return x.astype(F32).reshape(count, 8, wide)

    retain, unit, removal, key, value = [tiled(x) for x in (retain, unit, removal, key, value)]
    sub = lax.broadcasted_iota(jnp.int32, (count, 8, wide), 1)
    pulled = tiled(query)
    out = jnp.zeros_like(pulled)

    def segments(x):
        return head_sum(x.reshape(rows, wide), ones).reshape(count, 8, wide)

    for step in range(7, -1, -1):
        at = slice(step, step + 1)
        live = sub >= step
        out = out + jnp.where(live, segments(pulled * key[:, at]) * value[:, at], 0.0)
        new = pulled * retain[:, at] - segments(pulled * removal[:, at]) * unit[:, at]
        pulled = jnp.where(live, new, pulled)
    return pulled.reshape(rows, wide), out.reshape(rows, wide)


def states_kernel(*refs):
    pk, pv, pc, pd, pe, aq, ak, av, ac, ad, ae, moves, pulled, fresh = refs
    wide = WIDE
    diag_block = block_mask(wide, wide)
    ones = jnp.where(diag_block, 1.0, 0.0).astype(BF16)
    for g in range(pk.shape[1] // wide):
        s = slice(g * wide, (g + 1) * wide)
        passage, update = prefix_group(
            pk[:, s], pv[:, s], pc[:, s], pd[:, s], pe[:, s], ones, diag_block
        )
        for u in range(wide // LANES):
            lanes = slice(u * LANES, (u + 1) * LANES)
            moves[g * (wide // LANES) + u, :HSIZE] = passage[:, lanes]
            moves[g * (wide // LANES) + u, HSIZE:] = update[:, lanes]
        q, o = answer_group(aq[:, s], ak[:, s], av[:, s], ac[:, s], ad[:, s], ae[:, s], ones)
        pulled[:, s] = q
        fresh[:, s] = o


def chain_kernel(lengths, asked, moves, stage, states):
    shards = moves.shape[0]
    docs = lengths.shape[0]
    starts = []
    total = jnp.int32(0)
    for d in range(docs):
        starts.append(total)
        total = total + lengths[d]
    now = [None] * docs
    for d in range(docs):
        now[d] = moves[jnp.minimum(starts[d], shards - 1), HSIZE:]

    def step(j, now):
        out = []
        for d in range(docs):
            at = jnp.minimum(starts[d] + j, shards - 1)
            new = dot3(now[d], stack_heads(moves[at, :HSIZE])) + moves[at, HSIZE:]
            out.append(jnp.where(j < lengths[d], new, now[d]))
        return out

    now = lax.fori_loop(1, shards // 2, step, now)
    for d in range(docs):
        states[d] = now[d].astype(BF16)
    for q in range(shards):
        stage[q] = states[asked[q]]


def hidden_kernel(state, pulled, fresh, hidden):
    ones = jnp.where(block_mask(LANES, LANES), 1.0, 0.0).astype(BF16)
    for u in range(state.shape[0]):
        s = slice(u * LANES, (u + 1) * LANES)
        memory = stack_heads(state[u].astype(F32)).astype(BF16)
        x = pulled[:, s]
        high, low = split(x)
        lowest = (x - high.astype(F32) - low.astype(F32)).astype(BF16)
        out = mm(high, memory, NT) + (mm(low, memory, NT) + mm(lowest, memory, NT)) + fresh[:, s]
        centre = out - head_sum(out, ones) * (1.0 / HSIZE)
        spread = head_sum(centre * centre, ones) * (1.0 / HSIZE)
        hidden[:, s] = (centre * lax.rsqrt(spread + 1e-05)).astype(BF16)


def logits_kernel(offset, rows, ids, weight, stats, peak, mass, picked):
    step = pl.program_id(0)
    tile = weight.shape[1]

    @pl.when(step == 0)
    def _():
        peak[...] = jnp.full_like(peak, -jnp.inf)
        mass[...] = jnp.zeros_like(mass)
        picked[...] = jnp.zeros_like(picked)

    logits = jnp.dot(rows[...], weight[...], preferred_element_type=F32)
    column = lax.broadcasted_iota(jnp.int32, logits.shape, 1) + (offset[0] + step * tile)
    old = peak[:, :1]
    new = jnp.maximum(old, jnp.max(logits, 1, keepdims=True))
    add = jnp.sum(jnp.exp(logits - new), 1, keepdims=True)
    pick = jnp.sum(jnp.where(column == ids[:, :1], logits, 0.0), 1, keepdims=True)
    mass[...] = mass[...] * jnp.exp(old - new) + add
    picked[...] = picked[...] + pick
    peak[...] = jnp.broadcast_to(new, peak.shape)

    @pl.when(step == pl.num_programs(0) - 1)
    def _():
        lane = lax.broadcasted_iota(jnp.int32, stats.shape, 1)
        stats[...] = jnp.where(lane == 0, peak[...], jnp.where(lane == 1, mass[...], picked[...]))


VMEM = pl.BlockSpec(memory_space=pltpu.VMEM)
SMEM = pl.BlockSpec(memory_space=pltpu.SMEM)


def local(*args):
    prefix, answers = args[:5], args[5:11]
    doc_lengths, question_doc, choice_tokens, choice_lengths, head_weight = args[11:]
    shards = lax.axis_size("seq")
    my_index = lax.axis_index("seq")
    tok_rows, width = prefix[0].shape
    answers = [a.reshape(-1, width) for a in answers]
    rows = answers[0].shape[0]
    units = width // LANES
    copies = max(shards // units, 1)
    block = 2 * WIDE

    asked = lax.all_gather(question_doc, "seq", axis=0, tiled=True)
    part_ids = lax.all_gather(choice_tokens.reshape(-1), "seq", axis=0, tiled=True)

    moves, pulled, fresh = pl.pallas_call(
        states_kernel,
        grid=(width // block,),
        in_specs=[pl.BlockSpec((tok_rows, block), lambda i: (0, i))] * 5
        + [pl.BlockSpec((rows, block), lambda i: (0, i))] * 6,
        out_specs=[
            pl.BlockSpec((block // LANES, LANES, LANES), lambda i: (i, 0, 0)),
            pl.BlockSpec((rows, block), lambda i: (0, i)),
            pl.BlockSpec((rows, block), lambda i: (0, i)),
        ],
        out_shape=[
            jax.ShapeDtypeStruct((units, LANES, LANES), F32),
            jax.ShapeDtypeStruct((rows, width), F32),
            jax.ShapeDtypeStruct((rows, width), F32),
        ],
        compiler_params=pltpu.CompilerParams(vmem_limit_bytes=48 * 2**20),
        name="states",
    )(*prefix, *answers)
    if copies > 1:
        moves = jnp.repeat(moves, copies, axis=0)
    moves = lax.all_to_all(moves, "seq", split_axis=0, concat_axis=0, tiled=True)
    stage = pl.pallas_call(
        chain_kernel,
        in_specs=[SMEM, SMEM, VMEM],
        out_specs=VMEM,
        out_shape=jax.ShapeDtypeStruct((shards, HSIZE, LANES), BF16),
        scratch_shapes=[pltpu.VMEM((doc_lengths.shape[0], HSIZE, LANES), BF16)],
        name="chain",
    )(doc_lengths, asked, moves)
    state = lax.all_to_all(stage, "seq", split_axis=0, concat_axis=0, tiled=True)
    if copies > 1:
        state = state[::copies]
    hidden = pl.pallas_call(
        hidden_kernel,
        in_specs=[VMEM] * 3,
        out_specs=VMEM,
        out_shape=jax.ShapeDtypeStruct((rows, width), BF16),
        name="hidden",
    )(state, pulled, fresh)

    part_rows = lax.all_gather(hidden, "seq", axis=0, tiled=True)
    vocab_dev = head_weight.shape[1]
    tile = 512
    all_rows = shards * rows
    stats = pl.pallas_call(
        logits_kernel,
        grid=(vocab_dev // tile,),
        in_specs=[
            SMEM,
            pl.BlockSpec((all_rows, width), lambda i: (0, 0)),
            pl.BlockSpec((all_rows, LANES), lambda i: (0, 0)),
            pl.BlockSpec((width, tile), lambda i: (0, i)),
        ],
        out_specs=pl.BlockSpec((all_rows, LANES), lambda i: (0, 0)),
        out_shape=jax.ShapeDtypeStruct((all_rows, LANES), F32),
        scratch_shapes=[pltpu.VMEM((all_rows, LANES), F32)] * 3,
        compiler_params=pltpu.CompilerParams(vmem_limit_bytes=48 * 2**20),
        name="logits",
    )(
        (my_index * vocab_dev)[None],
        part_rows,
        jnp.broadcast_to(part_ids[:, None], (all_rows, LANES)),
        head_weight,
    )
    small = stats[:, :3].T.reshape(3, shards, rows).transpose(1, 0, 2)
    parts = lax.all_to_all(small, "seq", split_axis=0, concat_axis=0, tiled=True)
    peak, mass, picked = parts[:, 0], parts[:, 1], parts[:, 2]
    top = jnp.max(peak, 0)
    total = top + jnp.log(jnp.sum(mass * jnp.exp(peak - top[None, :]), 0))
    logprob = (jnp.sum(picked, 0) - total).reshape(choice_tokens.shape)
    inside = (
        jnp.arange(choice_tokens.shape[2], dtype=jnp.int32)[None, None, :]
        < choice_lengths[:, :, None]
    )
    return jnp.sum(jnp.where(inside, logprob, 0.0), -1) / choice_lengths.astype(F32)


def solution(mesh):
    token = P(("group", "seq"), None)
    choice = P(("group", "seq"), None, None, None)
    placed = (token,) * 5 + (choice,) * 6
    placed += (
        P("group"),
        P(("group", "seq")),
        P(("group", "seq"), None, None),
        P(("group", "seq"), None),
        P(None, "seq"),
    )
    return jax.shard_map(
        local, mesh=mesh, in_specs=placed, out_specs=P(("group", "seq"), None), check_vma=False
    )
```

time: 1480 us -> 236 us (0.16)
  other arithmetic: 1010 us -> 0.81 us
  starting transfers between devices: 208 us -> 7.42 us
  Pallas kernels: 0 us -> 107 us
  matrix products: 55.8 us -> 0 us
  local copies, waits for them, and re-layouts: 60.8 us -> 18 us
  waiting for transfers between devices: 82.5 us -> 39.9 us
    reduce_sum x279 -> x2, other arithmetic: 345 us -> 0.21 us  [the longest x1 0.18 us: local(): jnp.sum(jnp.where(inside, logprob, 0.0), -1) / choice_lengths.astype(F32)]
    scatter-add x136 -> x0, other arithmetic: 331 us -> none  [the longest x128 317 us: block_step(): states = states.at[1].add(value_now[:, :, None] * key_now[:, None, :])]
    sub x137 -> x1, other arithmetic: 260 us -> 0.01 us  [local(): logprob = (jnp.sum(picked, 0) - total).reshape(choice_tokens.shape)]
    ppermute x15 -> x0, starting transfers between devices: 197 us -> none  [from_behind(): return lax.ppermute(block, axis, route)]
    pallas_call x0 -> x4, Pallas kernels: none -> 107 us  [the longest x1 75.4 us: local(): pl.pallas_call(states_kernel, grid=(width // block,), in_specs=[pl.BlockS...]
    dot_general x18 -> x0, matrix products: 55.8 us -> none  [the longest x15 32.5 us: compose(): jnp.einsum('hvk,hkj->hvj', first_part, second_part, precision=lax.Precisi...]
    convert_element_type x23 -> x0, other arithmetic: 45 us -> none  [the longest x20 42.5 us: split_heads(): tensor.astype(jnp.float32)]
    convert_element_type x554 -> x0, local copies, waits for them, and re-layouts: 40.9 us -> none  [the longest x552 39.9 us: split_heads(): tensor.astype(jnp.float32)]
  transfers between devices with their start and end apart: 20 -> 2, of which waited for: 19 -> 1; matrix products, arithmetic and copies ran while one was open for 7% -> 1% of each run, Pallas kernels for 0% -> 0%
where the time goes in v1:
time: 236 us; the launch traced here: 235 us
  Pallas kernels  107 us (45%)
  blocking collectives  47 us (20%)
  waiting for transfers between devices  39.9 us (17%)
  local copies, waits for them, and re-layouts  18 us (8%)
  between operations  14.8 us (6%)
  starting transfers between devices  7.42 us (3%)
    pallas_call x1, Pallas kernels, local(): pl.pallas_call(states_kernel, grid=(width // block,), in_specs=[pl.BlockS...  75.4 us
    all_gather x1, waiting for transfers between devices, local(): part_rows = lax.all_gather(hidden, 'seq', axis=0, tiled=True)  39.8 us
    unnamed x1, blocking collectives  22.8 us
    pallas_call x1, Pallas kernels, local(): pl.pallas_call(logits_kernel, grid=(vocab_dev // tile,), in_specs=[SMEM,...  20.1 us
    unnamed x37, local copies, waits for them, and re-layouts  16.8 us
    all_to_all x1, blocking collectives, local(): lax.all_to_all(stage, 'seq', split_axis=0, concat_axis=0, tiled=True)  14.2 us
    all_to_all x1, blocking collectives, local(): lax.all_to_all(small, 'seq', split_axis=0, concat_axis=0, tiled=True)  9.91 us
    pallas_call x1, Pallas kernels, local(): pl.pallas_call(hidden_kernel, in_specs=[VMEM] * 3, out_specs=VMEM, out_sh...  7.98 us
  transfers between devices with their start and end apart: 2, of which 1 were waited for; matrix products, arithmetic and copies ran while one was open for 1% of the time, Pallas kernels for 0%

profile of v1, /device:TPU:0, one launch (start us, length us, event | category | flops | bytes accessed | tf_op | source)
XLA Modules:
  0.0 235.1 jit_solution(8484000225489361540)
XLA Ops:
  6.5 1.1 copy-done.1
  7.6 1.0 copy-done.2
  8.6 1.0 copy-done.3
  9.7 1.0 copy-done.4
  10.7 1.0 copy-done.5
  11.8 0.9 copy-done.8
  12.7 0.9 copy-done.9
  13.6 0.9 copy-done.10
  14.5 0.9 copy-done.11
  15.4 0.9 copy-done.12
  16.3 0.9 copy-done.13
  17.2 75.4 %states.1 = (f32[16,128,128]{2,1,0:T(8,128)}, f32[32,2048]{1,0:T(8,128)S(1)}, f32[32,2048]{1,0:T(8,128)S(1)}) custom-call(bf16[128,2048]{1,0:T(8,128)(2,1)S(1)} %copy-done.1, bf16[128,2048]{1,0:T(8,128)(2,1)S(1)} %copy-done.2, bf16[128,2048]{1,0:T(8,128)(2,1)S(1)} %copy-done.3, bf16[128,2048]{1,0:T(8,128)(2,1)S(1)} %copy-done.4, ...), custom_call_target="tpu_custom_call" | custom-call | tf_op jit(solution)/shard_map/states/pallas_call | solution.py:275
  94.0 7.4 %all-to-all-start = ((f32[16,128,128]{2,1,0:T(8,128)}), f32[16,128,128]{2,1,0:T(8,128)S(1)}, u32[]{:S(2)}, u32[]{:S(2)}) async-start(f32[16,128,128]{2,1,0:T(8,128)} %get-tuple-element.8), calls=%async_computation | async-start | bytes 2097152 | tf_op jit(solution)/shard_map/all_to_all | solution.py:295
  101.5 0.8 reshape.119
  102.9 1.2 dynamic-slice
  105.8 22.8 %all-reduce.2 = (s32[16]{0:T(128)}, s32[512]{0:T(512)S(1)}) all-reduce(s32[16]{0:T(128)S(1)} %dynamic-update-slice, s32[512]{0:T(512)S(1)} %dynamic-update-slice.1), channel_id=1, replica_groups=mesh['group'=2,'seq'=16] {'seq'}, use_global_device_ids=true, to_apply=%add | all-reduce | flops 528 | bytes 4224
  128.7 1.0 copy-done.14
  129.6 3.7 %chain.1 = bf16[16,64,128]{2,1,0:T(8,128)(2,1)} custom-call(s32[4]{0:T(128)} %lengths.1, s32[16]{0:T(128)} %get-tuple-element.11.asked, f32[16,128,128]{2,1,0:T(8,128)} %copy-done.14), custom_call_target="tpu_custom_call" | custom-call | tf_op jit(solution)/shard_map/chain/pallas_call | solution.py:296
  133.4 14.2 %all_to_all.15.state = bf16[16,64,128]{2,1,0:T(8,128)(2,1)} all-to-all(bf16[16,64,128]{2,1,0:T(8,128)(2,1)} %chain.1), channel_id=1, replica_groups=mesh['group'=2,'seq'=16] {'seq'}, dimensions={0} | all-to-all | bytes 524288 | tf_op jit(solution)/shard_map/all_to_all | solution.py:304
  147.6 8.0 %hidden.1 = bf16[32,2048]{1,0:T(8,128)(2,1)} custom-call(bf16[16,64,128]{2,1,0:T(8,128)(2,1)} %all_to_all.15.state, f32[32,2048]{1,0:T(8,128)} %copy-done.6, f32[32,2048]{1,0:T(8,128)} %copy-done.7), custom_call_target="tpu_custom_call" | custom-call | tf_op jit(solution)/shard_map/hidden/pallas_call | solution.py:307
  155.6 39.8 %all-gather.2.cloned.1.call-done.rows = bf16[512,2048]{1,0:T(8,128)(2,1)} async-done(((bf16[32,2048]{1,0:T(8,128)(2,1)}), bf16[512,2048]{1,0:T(8,128)(2,1)}) %all-gather.2.cloned.1.call-update) | async-done | bytes 2097168 | tf_op jit(solution)/shard_map/all_gather | solution.py:315
  195.6 1.6 copy-done
  197.2 20.1 %logits.1 = f32[512,128]{1,0:T(8,128)S(1)} custom-call(s32[1]{0:T(128)} %bitcast.1.offset, bf16[512,2048]{1,0:T(8,128)(2,1)S(1)} %copy-done, s32[512,128]{1,0:T(8,128)S(1)} %broadcast_in_dim.8.ids, bf16[2048,4096]{1,0:T(8,128)(2,1)} %weight.1), custom_call_target="tpu_custom_call" | custom-call | tf_op jit(solution)/shard_map/logits/pallas_call | solution.py:319
  217.5 9.9 %all_to_all.16 = f32[16,3,32]{2,1,0:T(4,128)S(1)} all-to-all(f32[16,3,32]{2,1,0:T(4,128)S(1)} %bitcast.30), channel_id=1, replica_groups=mesh['group'=2,'seq'=16] {'seq'}, dimensions={0} | all-to-all | bytes 12288 | tf_op jit(solution)/shard_map/all_to_all | solution.py:340
  (35 shorter events, 3.7 us)
Async XLA Ops:
  6.5 221.0 %copy-start.15 = (s32[1,4]{1,0:T(1,128)S(1)}, s32[1,4]{1,0:T(1,128)}, u32[]{:S(2)}) copy-start(s32[1,4]{1,0:T(1,128)} %param.30) | copy-start | bytes 52
  6.5 1.1 copy-start.1
  7.6 1.0 copy-start.2
  8.6 1.0 copy-start.3
  9.7 1.0 copy-start.4
  10.7 1.0 copy-start.5
  11.8 0.9 copy-start.8
  12.7 0.9 copy-start.9
  13.6 0.9 copy-start.10
  14.5 0.9 copy-start.11
  15.4 0.9 copy-start.12
  16.3 0.9 copy-start.13
  92.6 0.7 copy-start.6
  93.3 0.7 copy-start.7
  94.0 34.6 %all-to-all-start = ((f32[16,128,128]{2,1,0:T(8,128)}), f32[16,128,128]{2,1,0:T(8,128)S(1)}, u32[]{:S(2)}, u32[]{:S(2)}) async-start(f32[16,128,128]{2,1,0:T(8,128)} %get-tuple-element.8), calls=%async_computation | async-start | bytes 2097152 | tf_op jit(solution)/shard_map/all_to_all | solution.py:295
  101.4 94.0 %all-gather.2.cloned.1.call-start = ((), (), s32[]{:S(2)}) async-start(), calls=%async_computation.3 | async-start | bytes 2228224 | tf_op jit(solution)/shard_map/all_gather | solution.py:315
  128.7 1.0 copy-start.14
  195.6 1.6 copy-start
Sparse Core Ops, SparseCore 0:
  155.7 39.6 all-gather.1

commit v2 on v1

--- a/solution.py
+++ b/solution.py
@@ -186,7 +186,7 @@
         fresh[:, s] = o
 
 
-def chain_kernel(lengths, asked, moves, stage, states):
+def documents(lengths, moves):
     shards = moves.shape[0]
     docs = lengths.shape[0]
     starts = []
@@ -194,9 +194,7 @@
     for d in range(docs):
         starts.append(total)
         total = total + lengths[d]
-    now = [None] * docs
-    for d in range(docs):
-        now[d] = moves[jnp.minimum(starts[d], shards - 1), HSIZE:]
+    now = [moves[jnp.minimum(starts[d], shards - 1), HSIZE:] for d in range(docs)]
 
     def step(j, now):
         out = []
@@ -206,51 +204,220 @@
             out.append(jnp.where(j < lengths[d], new, now[d]))
         return out
 
-    now = lax.fori_loop(1, shards // 2, step, now)
-    for d in range(docs):
-        states[d] = now[d].astype(BF16)
+    return [x.astype(BF16) for x in lax.fori_loop(1, shards // 2, step, now)]
+
+
+def hidden_unit(state, x, fresh, ones):
+    memory = stack_heads(state.astype(F32)).astype(BF16)
+    high, low = split(x)
+    lowest = (x - high.astype(F32) - low.astype(F32)).astype(BF16)
+    out = mm(high, memory, NT) + (mm(low, memory, NT) + mm(lowest, memory, NT)) + fresh
+    centre = out - head_sum(out, ones) * (1.0 / HSIZE)
+    spread = head_sum(centre * centre, ones) * (1.0 / HSIZE)
+    return (centre * lax.rsqrt(spread + 1e-05)).astype(BF16)
+
+
+def score_kernel(
+    copies,
+    lengths,
+    choice_lengths,
+    meta,
+    moves,
+    pulled,
+    fresh,
+    weight,
+    scores,
+    meta_all,
+    moves_all,
+    stage,
+    state,
+    rows_all,
+    weight_all,
+    stats,
+    stats_all,
+    peak,
+    mass,
+    picked,
+    weight_sem,
+    meta_send,
+    meta_recv,
+    move_send,
+    move_recv,
+    state_send,
+    state_recv,
+    far_send,
+    far_recv,
+    mid_send,
+    mid_recv,
+    near_send,
+    near_recv,
+    stat_send,
+    stat_recv,
+):
+    shards = moves_all.shape[0]
+    me = lax.axis_index("seq")
+    rows = pulled.shape[0]
+    tiles, _, tile = weight_all.shape
+
+    def fetch(i):
+        return pltpu.make_async_copy(
+            weight.at[:, pl.ds(i * tile, tile)], weight_all.at[i], weight_sem.at[i]
+        )
+
+    for i in range(tiles):
+        fetch(i).start()
+
+    def send(source, target, send_sem, recv_sem, dest):
+        copy = pltpu.make_async_remote_copy(
+            src_ref=source,
+            dst_ref=target,
+            send_sem=send_sem,
+            recv_sem=recv_sem,
+            device_id={"seq": dest},
+            device_id_type=pl.DeviceIdType.MESH,
+        )
+        copy.start()
+        return copy
+
+    barrier = pltpu.get_barrier_semaphore()
+    for k in range(1, shards):
+        pl.semaphore_signal(
+            barrier,
+            inc=1,
+            device_id={"seq": lax.rem(me + k, shards)},
+            device_id_type=pl.DeviceIdType.MESH,
+        )
+    pl.semaphore_wait(barrier, shards - 1)
+
+    sent = []
+    arriving = []
+    for k in range(1, shards):
+        dest = lax.rem(me + k, shards)
+        small = send(meta, meta_all.at[me], meta_send.at[k], meta_recv.at[k], dest)
+        large = send(
+            moves.at[dest // copies], moves_all.at[me], move_send.at[k], move_recv.at[k], dest
+        )
+        arriving += [small, large]
+    meta_all[me] = meta[...]
+    moves_all[me] = moves[me // copies]
+    for copy in arriving:
+        copy.wait_recv()
+    sent += arriving
+
+    docs = documents(lengths, moves_all)
     for q in range(shards):
-        stage[q] = states[asked[q]]
-
-
-def hidden_kernel(state, pulled, fresh, hidden):
+        asked = jnp.broadcast_to(meta_all[q, rows : rows + 1, :], docs[0].shape)
+        chosen = docs[0].astype(F32)
+        for d in range(1, len(docs)):
+            chosen = jnp.where(asked == d, docs[d].astype(F32), chosen)
+        stage[q] = chosen.astype(BF16)
+    unit = me // copies
+    arriving = []
+    for k in range(copies, shards, copies):
+        dest = lax.rem(me + k, shards)
+        arriving.append(
+            send(stage.at[dest], state.at[unit], state_send.at[k], state_recv.at[k], dest)
+        )
+    state[unit] = stage[me]
+    for copy in arriving:
+        copy.wait_recv()
+    sent += arriving
+
     ones = jnp.where(block_mask(LANES, LANES), 1.0, 0.0).astype(BF16)
     for u in range(state.shape[0]):
         s = slice(u * LANES, (u + 1) * LANES)
-        memory = stack_heads(state[u].astype(F32)).astype(BF16)
-        x = pulled[:, s]
-        high, low = split(x)
-        lowest = (x - high.astype(F32) - low.astype(F32)).astype(BF16)
-        out = mm(high, memory, NT) + (mm(low, memory, NT) + mm(lowest, memory, NT)) + fresh[:, s]
-        centre = out - head_sum(out, ones) * (1.0 / HSIZE)
-        spread = head_sum(centre * centre, ones) * (1.0 / HSIZE)
-        hidden[:, s] = (centre * lax.rsqrt(spread + 1e-05)).astype(BF16)
-
-
-def logits_kernel(offset, rows, ids, weight, stats, peak, mass, picked):
-    step = pl.program_id(0)
-    tile = weight.shape[1]
-
-    @pl.when(step == 0)
-    def _():
-        peak[...] = jnp.full_like(peak, -jnp.inf)
-        mass[...] = jnp.zeros_like(mass)
-        picked[...] = jnp.zeros_like(picked)
-
-    logits = jnp.dot(rows[...], weight[...], preferred_element_type=F32)
-    column = lax.broadcasted_iota(jnp.int32, logits.shape, 1) + (offset[0] + step * tile)
-    old = peak[:, :1]
-    new = jnp.maximum(old, jnp.max(logits, 1, keepdims=True))
-    add = jnp.sum(jnp.exp(logits - new), 1, keepdims=True)
-    pick = jnp.sum(jnp.where(column == ids[:, :1], logits, 0.0), 1, keepdims=True)
-    mass[...] = mass[...] * jnp.exp(old - new) + add
-    picked[...] = picked[...] + pick
-    peak[...] = jnp.broadcast_to(new, peak.shape)
-
-    @pl.when(step == pl.num_programs(0) - 1)
-    def _():
-        lane = lax.broadcasted_iota(jnp.int32, stats.shape, 1)
-        stats[...] = jnp.where(lane == 0, peak[...], jnp.where(lane == 1, mass[...], picked[...]))
+        rows_all[me, :, s] = hidden_unit(state[u], pulled[:, s], fresh[:, s], ones)
+
+    hops = shards // 4
+    far, place = me // 4, lax.rem(me, 4)
+    mid_peer = me + 2 - 4 * (place // 2)
+    near_peer = me + 1 - 2 * lax.rem(me, 2)
+
+    def pass_on(slot, send_sems, recv_sems, k, dest):
+        return send(rows_all.at[slot], rows_all.at[slot], send_sems.at[k], recv_sems.at[k], dest)
+
+    fars = [None]
+    for d in range(1, hops):
+        dest = lax.rem(far + d, hops) * 4 + place
+        fars.append(pass_on(me, far_send, far_recv, d, dest))
+    mids = [pass_on(me, mid_send, mid_recv, 0, mid_peer)]
+    nears = [pass_on(me, near_send, near_recv, 0, near_peer)]
+    later = []
+
+    def from_mid(d):
+        mids[d].wait_recv()
+        slot = lax.rem(far - d + hops, hops) * 4 + lax.rem(place + 2, 4)
+        later.append(pass_on(slot, near_send, near_recv, hops + d, near_peer))
+
+    for d in range(1, hops):
+        fars[d].wait_recv()
+        slot = lax.rem(far - d + hops, hops) * 4 + place
+        mids.append(pass_on(slot, mid_send, mid_recv, d, mid_peer))
+        nears.append(pass_on(slot, near_send, near_recv, d, near_peer))
+        from_mid(d - 1)
+    from_mid(hops - 1)
+    for copy in nears + later:
+        copy.wait_recv()
+    sent += fars[1:] + mids + nears + later
+
+    total = shards * rows
+    peak[...] = jnp.full_like(peak, -jnp.inf)
+    mass[...] = jnp.zeros_like(mass)
+    picked[...] = jnp.zeros_like(picked)
+    first = me * (tiles * tile)
+
+    def score_tile(i, carry):
+        fetch(i).wait()
+        everyone = rows_all[...].reshape(total, rows_all.shape[2])
+        logits = jnp.dot(everyone, weight_all[i], preferred_element_type=F32)
+        ids = meta_all[:, :rows, :].reshape(total, LANES)
+        parts = [logits[:, p * LANES : (p + 1) * LANES] for p in range(tile // LANES)]
+        old = peak[...]
+        new = functools.reduce(jnp.maximum, parts, old)
+        add = mass[...] * jnp.exp(old - new)
+        pick = picked[...]
+        lane = lax.broadcasted_iota(jnp.int32, (total, LANES), 1) - ids
+        for p, part in enumerate(parts):
+            add = add + jnp.exp(part - new)
+            pick = pick + jnp.where(lane == -(first + i * tile + p * LANES), part, 0.0)
+        peak[...] = new
+        mass[...] = add
+        picked[...] = pick
+        return carry
+
+    lax.fori_loop(0, tiles, score_tile, 0)
+    top = jnp.max(peak[...], 1, keepdims=True)
+    summed = jnp.sum(mass[...] * jnp.exp(peak[...] - top), 1, keepdims=True)
+    chosen = jnp.sum(picked[...], 1, keepdims=True)
+    lane = lax.broadcasted_iota(jnp.int32, (total, LANES), 1)
+    packed = jnp.where(lane == 0, top, jnp.where(lane == 1, summed, chosen))
+    stats[...] = packed.reshape(shards, rows, LANES)
+
+    arriving = []
+    for k in range(1, shards):
+        dest = lax.rem(me + k, shards)
+        arriving.append(
+            send(stats.at[dest], stats_all.at[me], stat_send.at[k], stat_recv.at[k], dest)
+        )
+    stats_all[me] = stats[me]
+    for copy in arriving:
+        copy.wait_recv()
+    sent += arriving
+    tops = stats_all[:, :, 0:1]
+    overall = jnp.max(tops, 0)
+    masses = jnp.sum(stats_all[:, :, 1:2] * jnp.exp(tops - overall[None]), 0)
+    logprob = jnp.sum(stats_all[:, :, 2:3], 0) - (overall + jnp.log(masses))
+    logprob = jnp.broadcast_to(logprob, (rows, LANES))
+    slots = rows // choice_lengths.shape[1]
+    spot = lax.broadcasted_iota(jnp.int32, (slots, LANES), 0)
+    for c in range(choice_lengths.shape[1]):
+        count = choice_lengths[0, c]
+        mine = jnp.where(spot < count, logprob[c * slots : (c + 1) * slots], 0.0)
+        scores[c : c + 1, :] = jnp.sum(mine, 0, keepdims=True) / jnp.full(
+            (1, LANES), count, jnp.int32
+        ).astype(F32)
+    for copy in sent:
+        copy.wait_send()
 
 
 VMEM = pl.BlockSpec(memory_space=pltpu.VMEM)
@@ -268,9 +435,6 @@
     units = width // LANES
     copies = max(shards // units, 1)
     block = 2 * WIDE
-
-    asked = lax.all_gather(question_doc, "seq", axis=0, tiled=True)
-    part_ids = lax.all_gather(choice_tokens.reshape(-1), "seq", axis=0, tiled=True)
 
     moves, pulled, fresh = pl.pallas_call(
         states_kernel,
@@ -287,66 +451,44 @@
             jax.ShapeDtypeStruct((rows, width), F32),
             jax.ShapeDtypeStruct((rows, width), F32),
         ],
-        compiler_params=pltpu.CompilerParams(vmem_limit_bytes=48 * 2**20),
+        compiler_params=pltpu.CompilerParams(vmem_limit_bytes=60 * 2**20),
         name="states",
     )(*prefix, *answers)
-    if copies > 1:
-        moves = jnp.repeat(moves, copies, axis=0)
-    moves = lax.all_to_all(moves, "seq", split_axis=0, concat_axis=0, tiled=True)
-    stage = pl.pallas_call(
-        chain_kernel,
-        in_specs=[SMEM, SMEM, VMEM],
-        out_specs=VMEM,
-        out_shape=jax.ShapeDtypeStruct((shards, HSIZE, LANES), BF16),
-        scratch_shapes=[pltpu.VMEM((doc_lengths.shape[0], HSIZE, LANES), BF16)],
-        name="chain",
-    )(doc_lengths, asked, moves)
-    state = lax.all_to_all(stage, "seq", split_axis=0, concat_axis=0, tiled=True)
-    if copies > 1:
-        state = state[::copies]
-    hidden = pl.pallas_call(
-        hidden_kernel,
-        in_specs=[VMEM] * 3,
-        out_specs=VMEM,
-        out_shape=jax.ShapeDtypeStruct((rows, width), BF16),
-        name="hidden",
-    )(state, pulled, fresh)
-
-    part_rows = lax.all_gather(hidden, "seq", axis=0, tiled=True)
+    meta = jnp.concatenate(
+        [choice_tokens.reshape(-1), jnp.broadcast_to(question_doc, (8,))]
+    )
+    meta = jnp.broadcast_to(meta[:, None], (rows + 8, LANES))
     vocab_dev = head_weight.shape[1]
     tile = 512
     all_rows = shards * rows
-    stats = pl.pallas_call(
-        logits_kernel,
-        grid=(vocab_dev // tile,),
-        in_specs=[
-            SMEM,
-            pl.BlockSpec((all_rows, width), lambda i: (0, 0)),
-            pl.BlockSpec((all_rows, LANES), lambda i: (0, 0)),
-            pl.BlockSpec((width, tile), lambda i: (0, i)),
-        ],
-        out_specs=pl.BlockSpec((all_rows, LANES), lambda i: (0, 0)),
-        out_shape=jax.ShapeDtypeStruct((all_rows, LANES), F32),
-        scratch_shapes=[pltpu.VMEM((all_rows, LANES), F32)] * 3,
-        compiler_params=pltpu.CompilerParams(vmem_limit_bytes=48 * 2**20),
-        name="logits",
-    )(
-        (my_index * vocab_dev)[None],
-        part_rows,
-        jnp.broadcast_to(part_ids[:, None], (all_rows, LANES)),
-        head_weight,
-    )
-    small = stats[:, :3].T.reshape(3, shards, rows).transpose(1, 0, 2)
-    parts = lax.all_to_all(small, "seq", split_axis=0, concat_axis=0, tiled=True)
-    peak, mass, picked = parts[:, 0], parts[:, 1], parts[:, 2]
-    top = jnp.max(peak, 0)
-    total = top + jnp.log(jnp.sum(mass * jnp.exp(peak - top[None, :]), 0))
-    logprob = (jnp.sum(picked, 0) - total).reshape(choice_tokens.shape)
-    inside = (
-        jnp.arange(choice_tokens.shape[2], dtype=jnp.int32)[None, None, :]
-        < choice_lengths[:, :, None]
-    )
-    return jnp.sum(jnp.where(inside, logprob, 0.0), -1) / choice_lengths.astype(F32)
+    choices = choice_tokens.shape[1]
+    dma = pltpu.SemaphoreType.DMA
+    scores = pl.pallas_call(
+        functools.partial(score_kernel, copies),
+        in_specs=[SMEM, SMEM, VMEM, VMEM, VMEM, VMEM, pl.BlockSpec(memory_space=pl.ANY)],
+        out_specs=VMEM,
+        out_shape=jax.ShapeDtypeStruct((choices, LANES), F32),
+        scratch_shapes=[
+            pltpu.VMEM((shards, rows + 8, LANES), jnp.int32),
+            pltpu.VMEM((shards, LANES, LANES), F32),
+            pltpu.VMEM((shards, HSIZE, LANES), BF16),
+            pltpu.VMEM((units, HSIZE, LANES), BF16),
+            pltpu.VMEM((shards, rows, width), BF16),
+            pltpu.VMEM((vocab_dev // tile, width, tile), BF16),
+            pltpu.VMEM((shards, rows, LANES), F32),
+            pltpu.VMEM((shards, rows, LANES), F32),
+            pltpu.VMEM((all_rows, LANES), F32),
+            pltpu.VMEM((all_rows, LANES), F32),
+            pltpu.VMEM((all_rows, LANES), F32),
+            dma((vocab_dev // tile,)),
+        ]
+        + [dma((shards,))] * 14,
+        compiler_params=pltpu.CompilerParams(
+            vmem_limit_bytes=60 * 2**20, collective_id=0, has_side_effects=True
+        ),
+        name="score",
+    )(doc_lengths, choice_lengths, meta, moves, pulled, fresh, head_weight)
+    return scores[:, 0][None]
 
 
 def solution(mesh):

time: 236 us -> 177 us (0.75)
  Pallas kernels: 107 us -> 173 us
  blocking collectives: 47 us -> 0 us
  waiting for transfers between devices: 39.9 us -> 0 us
  local copies, waits for them, and re-layouts: 18 us -> 2.72 us
  between operations: 14.8 us -> 0.66 us
  starting transfers between devices: 7.42 us -> 0 us
    pallas_call x3 -> x1, Pallas kernels: 31.8 us -> 96.1 us  [local(): pl.pallas_call(functools.partial(score_kernel, copies), in_specs=[SMEM, S...]
    all_gather x1 -> x0, waiting for transfers between devices: 39.8 us -> none  [local(): part_rows = lax.all_gather(hidden, 'seq', axis=0, tiled=True)]
    all_to_all x2 -> x0, blocking collectives: 24.1 us -> none  [the longest x1 14.2 us: local(): lax.all_to_all(stage, 'seq', split_axis=0, concat_axis=0, tiled=True)]
    unnamed x1 -> x0, blocking collectives: 22.8 us -> none
    unnamed x37 -> x0, local copies, waits for them, and re-layouts: 16.8 us -> none
    all_to_all x1 -> x0, starting transfers between devices: 7.38 us -> none  [local(): lax.all_to_all(moves, 'seq', split_axis=0, concat_axis=0, tiled=True)]
  transfers between devices with their start and end apart: 2 -> 0, of which waited for: 1 -> 0; matrix products, arithmetic and copies ran while one was open for 1% -> 0% of each run, Pallas kernels for 0% -> 0%
where the time goes in v2:
time: 177 us; the launch traced here: 176 us
  Pallas kernels  173 us (98%)
  local copies, waits for them, and re-layouts  2.72 us (2%)
    pallas_call x1, Pallas kernels, local(): pl.pallas_call(functools.partial(score_kernel, copies), in_specs=[SMEM, S...  96.1 us
    pallas_call x1, Pallas kernels, local(): pl.pallas_call(states_kernel, grid=(width // block,), in_specs=[pl.BlockS...  77 us

profile of v2, /device:TPU:0, one launch (start us, length us, event | category | flops | bytes accessed | tf_op | source)
XLA Modules:
  0.0 176.4 jit_solution(11713517529501923514)
XLA Ops:
  0.7 0.8 reshape.22
  1.4 0.7 broadcast_in_dim.5.meta
  2.1 77.0 %states.1 = (f32[16,128,128]{2,1,0:T(8,128)}, f32[32,2048]{1,0:T(8,128)}, f32[32,2048]{1,0:T(8,128)}) custom-call(bf16[128,2048]{1,0:T(8,128)(2,1)} %refs_0_.1, bf16[128,2048]{1,0:T(8,128)(2,1)} %refs_1_.1, bf16[128,2048]{1,0:T(8,128)(2,1)} %refs_2_.1, bf16[128,2048]{1,0:T(8,128)(2,1)} %refs_3_.1, bf16[128,2048]{1,0:T(8,128)(2,1)} %refs_4_.1, ...), custom_call_target="tpu_custom_call" | custom-call | tf_op jit(solution)/shard_map/states/pallas_call | solution.py:439
  79.1 96.1 %score.1 = f32[4,128]{1,0:T(4,128)} custom-call(s32[4]{0:T(128)} %lengths.1, s32[1,4]{1,0:T(1,128)} %choice_lengths.1, s32[40,128]{1,0:T(8,128)} %broadcast_in_dim.5.meta, f32[16,128,128]{2,1,0:T(8,128)} %get-tuple-element.8.moves, f32[32,2048]{1,0:T(8,128)} %get-tuple-element.9.pulled, f32[32,2048]{1,0:T(8,128)} %get-tuple-element.10.fresh, ...), custom_call_target="tpu_custom_call" | custom-call | tf_op jit(solution)/shard_map/score/pallas_call | solution.py:466
  175.1 1.3 slice_reduce_fusion
  (1 shorter events, 0.0 us)

commit v3 on v2

--- a/solution.py
+++ b/solution.py
@@ -10,7 +10,6 @@
 HSIZE = 64
 LANES = 128
 WIDE = 256
-CHUNK = 16
 F32 = jnp.float32
 BF16 = jnp.bfloat16
 
@@ -32,6 +31,10 @@
 def dot3(a, b, dims=NN):
     ah, al = split(a)
     bh, bl = split(b)
+    rows = a.shape[0]
+    if dims != TN and rows % 16 == 0:
+        both = mm(jnp.concatenate([ah, al], 0), bh, dims)
+        return both[:rows] + (both[rows:] + mm(ah, bl, dims))
     return mm(ah, bh, dims) + (mm(al, bh, dims) + mm(ah, bl, dims))
 
 
@@ -43,8 +46,10 @@
 
 
 def head_sum(x, ones):
+    rows = x.shape[0]
     high, low = split(x)
-    return mm(high, ones, NN) + mm(low, ones, NN)
+    both = mm(jnp.concatenate([high, low], 0), ones, NN)
+    return both[:rows] + both[rows:]
 
 
 def stack_heads(x):
@@ -67,104 +72,88 @@
     return jnp.exp(-decay.astype(F32)), unit, unit * learn.astype(F32)
 
 
-def prefix_group(key, value, kappa, decay, learn, ones, diag_block):
+def merge(first, second):
+    gain_a, pulled_a, faded_a, keys_a = first
+    gain_b, pulled_b, faded_b, keys_b = second
+    seen = dot3(pulled_b, stack_heads(faded_a), NT)
+    moved = gain_a * pulled_b - dot3(seen, stack_heads(pulled_a))
+    hit = dot3(keys_a, stack_heads(pulled_b), NT)
+    kept = gain_b * keys_a - dot3(hit, stack_heads(faded_b))
+    return (
+        gain_a * gain_b,
+        jnp.concatenate([pulled_a, moved], 0),
+        jnp.concatenate([gain_b * faded_a, faded_b], 0),
+        jnp.concatenate([kept, keys_b], 0),
+    )
+
+
+def state_group(prefix, answers, ones, diag_block):
+    key, value, kappa, decay, learn = prefix
+    query, akey, avalue, akappa, adecay, alearn = answers
     rows, wide = key.shape
-    chunks = rows // CHUNK
-    retain, unit, removal = factors(kappa, decay, learn, ones)
-
-    def halves(x):
-        x = x.reshape(chunks, 2, 8, wide)
-        return [x[:, 0], x[:, 1]]
-
-    retain, unit, removal = halves(retain), halves(unit), halves(removal)
-    sub = lax.broadcasted_iota(jnp.int32, (chunks, 8, wide), 1)
-
-    def at(parts, step):
-        return parts[step // 8][:, step % 8 : step % 8 + 1, :]
-
-    def segments(x):
-        return head_sum(x.reshape(chunks * 8, wide), ones).reshape(chunks, 8, wide)
-
-    pushed = halves(key.astype(F32))
-    for step in range(1, CHUNK):
-        r, u, w = at(retain, step), at(unit, step), at(removal, step)
-        for half in range(step // 8 + 1):
-            if half * 8 >= step:
-                continue
-            x = pushed[half]
-            new = x * r - segments(x * u) * w
-            pushed[half] = new if step >= half * 8 + 8 else jnp.where(sub < step - half * 8, new, x)
-    pulled = list(unit)
-    for step in range(CHUNK - 2, -1, -1):
-        r, u, w = at(retain, step), at(unit, step), at(removal, step)
-        for half in range(2):
-            if half * 8 + 7 <= step:
-                continue
-            x = pulled[half]
-            new = x * r - segments(x * w) * u
-            pulled[half] = new if step < half * 8 else jnp.where(sub > step - half * 8, new, x)
-    tail = jnp.ones((chunks, 1, wide), F32)
-    faded = [None] * CHUNK
-    for step in range(CHUNK - 1, -1, -1):
-        faded[step] = at(removal, step) * tail
-        tail = tail * at(retain, step)
-
-    def joined(parts):
-        return jnp.concatenate([p.reshape(chunks, 1, 8, wide) for p in parts], 1).reshape(rows, wide)
-
-    def spread(items):
-        out = jnp.zeros((chunks, 8, wide), F32)
-        for spot, item in enumerate(items):
-            out = jnp.where(sub == spot, item, out)
-        return out
-
-    faded = joined([spread(faded[:8]), spread(faded[8:])])
-    pulled = joined(pulled)
-    pushed = joined(pushed)
-    eye = lax.broadcasted_iota(jnp.int32, (wide, wide), 0) == lax.broadcasted_iota(
-        jnp.int32, (wide, wide), 1
-    )
-    passage = None
-    keys = None
-    for c in range(chunks):
-        part = slice(c * CHUNK, (c + 1) * CHUNK)
-        low_rank = dot3(pulled[part], faded[part], TN)
-        whole = jnp.where(eye, tail[c], 0.0) - jnp.where(diag_block, low_rank, 0.0)
-        if c == 0:
-            passage = fold_heads(whole)
-            keys = pushed[part]
-        else:
-            moved = dot3(jnp.concatenate([passage, keys], 0), whole)
-            passage = moved[:HSIZE]
-            keys = jnp.concatenate([moved[HSIZE:], pushed[part]], 0)
+    arows = query.shape[0]
+    retain, unit, removal = factors(
+        jnp.concatenate([kappa, akappa], 0),
+        jnp.concatenate([decay, adecay], 0),
+        jnp.concatenate([learn, alearn], 0),
+        ones,
+    )
+
+    def tiled(x):
+        return x.reshape(-1, 8, wide)
+
+    tiles = rows // 8
+    aretain, aunit, aremoval = [tiled(x[rows:]) for x in (retain, unit, removal)]
+    retain, unit, removal = [tiled(x[:rows]) for x in (retain, unit, removal)]
+    akey, avalue = tiled(akey.astype(F32)), tiled(avalue.astype(F32))
+    sub = lax.broadcasted_iota(jnp.int32, (tiles, 8, wide), 1)
+    asub = sub[: arows // 8]
+    pushed = tiled(key.astype(F32))
+    pulled = unit
+    apulled = tiled(query.astype(F32))
+    out = jnp.zeros_like(apulled)
+    for t in range(8):
+        j = 7 - t
+        pt = slice(t, t + 1)
+        aj = slice(j, j + 1)
+        terms = [apulled * akey[:, aj], apulled * aremoval[:, aj]]
+        if t == 0:
+            terms = [x.reshape(-1, wide) for x in terms]
+            sums = head_sum(jnp.concatenate(terms, 0), ones)
+            got, gone = tiled(sums[:arows]), tiled(sums[arows:])
+        if t > 0:
+            pj = slice(7 - t, 8 - t)
+            terms = [pushed * unit[:, pt], pulled * removal[:, pj]] + terms
+            terms = [x.reshape(-1, wide) for x in terms]
+            sums = head_sum(jnp.concatenate(terms, 0), ones)
+            new = pushed * retain[:, pt] - tiled(sums[:rows]) * removal[:, pt]
+            pushed = jnp.where(sub < t, new, pushed)
+            new = pulled * retain[:, pj] - tiled(sums[rows : 2 * rows]) * unit[:, pj]
+            pulled = jnp.where(sub > 7 - t, new, pulled)
+            got = tiled(sums[2 * rows : 2 * rows + arows])
+            gone = tiled(sums[2 * rows + arows :])
+        live = asub >= j
+        out = out + jnp.where(live, got * avalue[:, aj], 0.0)
+        apulled = jnp.where(live, apulled * aretain[:, aj] - gone * aunit[:, aj], apulled)
+    gain = jnp.ones((tiles, 1, wide), F32)
+    faded = removal
+    for t in range(7, -1, -1):
+        faded = jnp.where(sub == t, removal * gain, faded)
+        gain = gain * retain[:, t : t + 1]
+    parts = [(gain[c], pulled[c], faded[c], pushed[c]) for c in range(tiles)]
+    while len(parts) > 1:
+        parts = [merge(parts[i], parts[i + 1]) for i in range(0, len(parts), 2)]
+    gain, pulled, faded, keys = parts[0]
+    low_rank = fold_heads(jnp.where(diag_block, dot3(pulled, faded, TN), 0.0))
+    eye = (
+        lax.broadcasted_iota(jnp.int32, (HSIZE, wide), 0)
+        == lax.broadcasted_iota(jnp.int32, (HSIZE, wide), 1) % HSIZE
+    )
+    passage = jnp.where(eye, gain, 0.0) - low_rank
     high, low = split(keys)
     outer = mm(value, high, TN) + mm(value, low, TN)
-    return passage, fold_heads(jnp.where(diag_block, outer, 0.0))
-
-
-def answer_group(query, key, value, kappa, decay, learn, ones):
-    rows, wide = query.shape
-    count = rows // 8
-    retain, unit, removal = factors(kappa, decay, learn, ones)
-
-    def tiled(x):
-        return x.astype(F32).reshape(count, 8, wide)
-
-    retain, unit, removal, key, value = [tiled(x) for x in (retain, unit, removal, key, value)]
-    sub = lax.broadcasted_iota(jnp.int32, (count, 8, wide), 1)
-    pulled = tiled(query)
-    out = jnp.zeros_like(pulled)
-
-    def segments(x):
-        return head_sum(x.reshape(rows, wide), ones).reshape(count, 8, wide)
-
-    for step in range(7, -1, -1):
-        at = slice(step, step + 1)
-        live = sub >= step
-        out = out + jnp.where(live, segments(pulled * key[:, at]) * value[:, at], 0.0)
-        new = pulled * retain[:, at] - segments(pulled * removal[:, at]) * unit[:, at]
-        pulled = jnp.where(live, new, pulled)
-    return pulled.reshape(rows, wide), out.reshape(rows, wide)
+    update = fold_heads(jnp.where(diag_block, outer, 0.0))
+    return passage, update, apulled.reshape(arows, wide), out.reshape(arows, wide)
 
 
 def states_kernel(*refs):
@@ -174,14 +163,16 @@
     ones = jnp.where(diag_block, 1.0, 0.0).astype(BF16)
     for g in range(pk.shape[1] // wide):
         s = slice(g * wide, (g + 1) * wide)
-        passage, update = prefix_group(
-            pk[:, s], pv[:, s], pc[:, s], pd[:, s], pe[:, s], ones, diag_block
+        passage, update, q, o = state_group(
+            [r[:, s] for r in (pk, pv, pc, pd, pe)],
+            [r[:, s] for r in (aq, ak, av, ac, ad, ae)],
+            ones,
+            diag_block,
         )
         for u in range(wide // LANES):
             lanes = slice(u * LANES, (u + 1) * LANES)
             moves[g * (wide // LANES) + u, :HSIZE] = passage[:, lanes]
             moves[g * (wide // LANES) + u, HSIZE:] = update[:, lanes]
-        q, o = answer_group(aq[:, s], ak[:, s], av[:, s], ac[:, s], ad[:, s], ae[:, s], ones)
         pulled[:, s] = q
         fresh[:, s] = o
 

time: 177 us -> 161 us (0.910)
  Pallas kernels: 173 us -> 157 us
    pallas_call x1, Pallas kernels: 77 us -> 62.3 us  [local(): pl.pallas_call(states_kernel, grid=(width // block,), in_specs=[pl.BlockS...]
where the time goes in v3:
time: 161 us
  Pallas kernels  157 us (98%)
  local copies, waits for them, and re-layouts  2.72 us (2%)
    pallas_call x1, Pallas kernels, local(): pl.pallas_call(functools.partial(score_kernel, copies), in_specs=[SMEM, S...  95.1 us
    pallas_call x1, Pallas kernels, local(): pl.pallas_call(states_kernel, grid=(width // block,), in_specs=[pl.BlockS...  62.3 us

profile of v3, /device:TPU:0, one launch (start us, length us, event | category | flops | bytes accessed | tf_op | source)
XLA Modules:
  0.0 160.8 jit_solution(12574733464185281915)
XLA Ops:
  0.7 0.8 reshape.22
  1.4 0.7 broadcast_in_dim.5.meta
  2.1 62.3 %states.1 = (f32[16,128,128]{2,1,0:T(8,128)}, f32[32,2048]{1,0:T(8,128)}, f32[32,2048]{1,0:T(8,128)}) custom-call(bf16[128,2048]{1,0:T(8,128)(2,1)} %refs_0_.1, bf16[128,2048]{1,0:T(8,128)(2,1)} %refs_1_.1, bf16[128,2048]{1,0:T(8,128)(2,1)} %refs_2_.1, bf16[128,2048]{1,0:T(8,128)(2,1)} %refs_3_.1, bf16[128,2048]{1,0:T(8,128)(2,1)} %refs_4_.1, ...), custom_call_target="tpu_custom_call" | custom-call | tf_op jit(solution)/shard_map/states/pallas_call | solution.py:430
  64.4 95.1 %score.1 = f32[4,128]{1,0:T(4,128)} custom-call(s32[4]{0:T(128)} %lengths.1, s32[1,4]{1,0:T(1,128)} %choice_lengths.1, s32[40,128]{1,0:T(8,128)} %broadcast_in_dim.5.meta, f32[16,128,128]{2,1,0:T(8,128)} %get-tuple-element.8.moves, f32[32,2048]{1,0:T(8,128)} %get-tuple-element.9.pulled, f32[32,2048]{1,0:T(8,128)} %get-tuple-element.10.fresh, ...), custom_call_target="tpu_custom_call" | custom-call | tf_op jit(solution)/shard_map/score/pallas_call | solution.py:457
  159.5 1.3 slice_reduce_fusion
  (1 shorter events, 0.0 us)

commit v4 on v3

--- a/solution.py
+++ b/solution.py
@@ -72,18 +72,54 @@
     return jnp.exp(-decay.astype(F32)), unit, unit * learn.astype(F32)
 
 
-def merge(first, second):
-    gain_a, pulled_a, faded_a, keys_a = first
-    gain_b, pulled_b, faded_b, keys_b = second
-    seen = dot3(pulled_b, stack_heads(faded_a), NT)
-    moved = gain_a * pulled_b - dot3(seen, stack_heads(pulled_a))
-    hit = dot3(keys_a, stack_heads(pulled_b), NT)
-    kept = gain_b * keys_a - dot3(hit, stack_heads(faded_b))
+def stack_split(x):
+    heads = x.shape[1] // HSIZE
+    lane = lax.broadcasted_iota(jnp.int32, (1, x.shape[1]), 1) // HSIZE
+    keep = [jnp.where(lane == h, 1.0, 0.0).astype(BF16) for h in range(heads)]
+    return [jnp.concatenate([part * k for k in keep], 0) for part in split(x)]
+
+
+def dot_stacked(a, stacked, dims):
+    rows = a.shape[0]
+    both = mm(jnp.concatenate(split(a), 0), stacked[0], dims)
+    return both[:rows] + (both[rows:] + mm(a.astype(BF16), stacked[1], dims))
+
+
+def merge(gain, pulled, faded, keys, size):
+    rows, wide = pulled.shape
+    pairs = rows // (2 * size)
+    half = rows // 2
+
+    def parted(x):
+        x = x.reshape(pairs, 2, size, wide)
+        return x[:, 0].reshape(half, wide), x[:, 1].reshape(half, wide)
+
+    def joined(x, y):
+        shape = (pairs, 1, size, wide)
+        return jnp.concatenate([x.reshape(shape), y.reshape(shape)], 1).reshape(rows, wide)
+
+    def scaled(x, by):
+        return (x.reshape(pairs, size, wide) * by).reshape(half, wide)
+
+    gain = gain.reshape(pairs, 2, 1, wide)
+    gain_a, gain_b = gain[:, 0], gain[:, 1]
+    pulled_a, pulled_b = parted(pulled)
+    faded_a, faded_b = parted(faded)
+    keys_a, keys_b = parted(keys)
+    across = (half, half * (wide // HSIZE))
+    same = (
+        lax.broadcasted_iota(jnp.int32, across, 0) // size
+        == lax.broadcasted_iota(jnp.int32, across, 1) % half // size
+    )
+    seen = jnp.where(same, dot_stacked(pulled_b, stack_split(faded_a), NT), 0.0)
+    moved = scaled(pulled_b, gain_a) - dot_stacked(seen, stack_split(pulled_a), NN)
+    hit = jnp.where(same, dot_stacked(keys_a, stack_split(pulled_b), NT), 0.0)
+    kept = scaled(keys_a, gain_b) - dot_stacked(hit, stack_split(faded_b), NN)
     return (
         gain_a * gain_b,
-        jnp.concatenate([pulled_a, moved], 0),
-        jnp.concatenate([gain_b * faded_a, faded_b], 0),
-        jnp.concatenate([kept, keys_b], 0),
+        joined(pulled_a, moved),
+        joined(scaled(faded_a, gain_b), faded_b),
+        joined(kept, keys_b),
     )
 
 
@@ -140,10 +176,12 @@
     for t in range(7, -1, -1):
         faded = jnp.where(sub == t, removal * gain, faded)
         gain = gain * retain[:, t : t + 1]
-    parts = [(gain[c], pulled[c], faded[c], pushed[c]) for c in range(tiles)]
-    while len(parts) > 1:
-        parts = [merge(parts[i], parts[i + 1]) for i in range(0, len(parts), 2)]
-    gain, pulled, faded, keys = parts[0]
+    pulled, faded, keys = [x.reshape(rows, wide) for x in (pulled, faded, pushed)]
+    size = 8
+    while size < rows:
+        gain, pulled, faded, keys = merge(gain, pulled, faded, keys, size)
+        size *= 2
+    gain = gain.reshape(1, wide)
     low_rank = fold_heads(jnp.where(diag_block, dot3(pulled, faded, TN), 0.0))
     eye = (
         lax.broadcasted_iota(jnp.int32, (HSIZE, wide), 0)

time: 161 us -> 136 us (0.84)
  Pallas kernels: 157 us -> 133 us
    pallas_call x1, Pallas kernels: 62.3 us -> 37.6 us  [local(): pl.pallas_call(states_kernel, grid=(width // block,), in_specs=[pl.BlockS...]
where the time goes in v4:
time: 136 us
  Pallas kernels  133 us (98%)
  local copies, waits for them, and re-layouts  2.72 us (2%)
    pallas_call x1, Pallas kernels, local(): pl.pallas_call(functools.partial(score_kernel, copies), in_specs=[SMEM, S...  95.1 us
    pallas_call x1, Pallas kernels, local(): pl.pallas_call(states_kernel, grid=(width // block,), in_specs=[pl.BlockS...  37.6 us

profile of v4, /device:TPU:0, one launch (start us, length us, event | category | flops | bytes accessed | tf_op | source)
XLA Modules:
  0.0 136.1 jit_solution(14976986538704485372)
XLA Ops:
  0.7 0.8 reshape.22
  1.4 0.7 broadcast_in_dim.5.meta
  2.1 37.6 %states.1 = (f32[16,128,128]{2,1,0:T(8,128)}, f32[32,2048]{1,0:T(8,128)}, f32[32,2048]{1,0:T(8,128)}) custom-call(bf16[128,2048]{1,0:T(8,128)(2,1)} %refs_0_.1, bf16[128,2048]{1,0:T(8,128)(2,1)} %refs_1_.1, bf16[128,2048]{1,0:T(8,128)(2,1)} %refs_2_.1, bf16[128,2048]{1,0:T(8,128)(2,1)} %refs_3_.1, bf16[128,2048]{1,0:T(8,128)(2,1)} %refs_4_.1, ...), custom_call_target="tpu_custom_call" | custom-call | tf_op jit(solution)/shard_map/states/pallas_call | solution.py:468
  39.7 95.1 %score.1 = f32[4,128]{1,0:T(4,128)} custom-call(s32[4]{0:T(128)} %lengths.1, s32[1,4]{1,0:T(1,128)} %choice_lengths.1, s32[40,128]{1,0:T(8,128)} %broadcast_in_dim.5.meta, f32[16,128,128]{2,1,0:T(8,128)} %get-tuple-element.8.moves, f32[32,2048]{1,0:T(8,128)} %get-tuple-element.9.pulled, f32[32,2048]{1,0:T(8,128)} %get-tuple-element.10.fresh, ...), custom_call_target="tpu_custom_call" | custom-call | tf_op jit(solution)/shard_map/score/pallas_call | solution.py:495
  134.8 1.3 slice_reduce_fusion
  (1 shorter events, 0.0 us)

commit v5 on v4

--- a/solution.py
+++ b/solution.py
@@ -194,27 +194,6 @@
     return passage, update, apulled.reshape(arows, wide), out.reshape(arows, wide)
 
 
-def states_kernel(*refs):
-    pk, pv, pc, pd, pe, aq, ak, av, ac, ad, ae, moves, pulled, fresh = refs
-    wide = WIDE
-    diag_block = block_mask(wide, wide)
-    ones = jnp.where(diag_block, 1.0, 0.0).astype(BF16)
-    for g in range(pk.shape[1] // wide):
-        s = slice(g * wide, (g + 1) * wide)
-        passage, update, q, o = state_group(
-            [r[:, s] for r in (pk, pv, pc, pd, pe)],
-            [r[:, s] for r in (aq, ak, av, ac, ad, ae)],
-            ones,
-            diag_block,
-        )
-        for u in range(wide // LANES):
-            lanes = slice(u * LANES, (u + 1) * LANES)
-            moves[g * (wide // LANES) + u, :HSIZE] = passage[:, lanes]
-            moves[g * (wide // LANES) + u, HSIZE:] = update[:, lanes]
-        pulled[:, s] = q
-        fresh[:, s] = o
-
-
 def documents(lengths, moves):
     shards = moves.shape[0]
     docs = lengths.shape[0]
@@ -251,38 +230,43 @@
     lengths,
     choice_lengths,
     meta,
-    moves,
-    pulled,
-    fresh,
-    weight,
-    scores,
-    meta_all,
-    moves_all,
-    stage,
-    state,
-    rows_all,
-    weight_all,
-    stats,
-    stats_all,
-    peak,
-    mass,
-    picked,
-    weight_sem,
-    meta_send,
-    meta_recv,
-    move_send,
-    move_recv,
-    state_send,
-    state_recv,
-    far_send,
-    far_recv,
-    mid_send,
-    mid_recv,
-    near_send,
-    near_recv,
-    stat_send,
-    stat_recv,
+    *refs,
 ):
+    (
+        prefix,
+        answers,
+        weight,
+        scores,
+        moves,
+        pulled,
+        fresh,
+        meta_all,
+        moves_all,
+        stage,
+        state,
+        rows_all,
+        weight_all,
+        stats,
+        stats_all,
+        peak,
+        mass,
+        picked,
+        weight_sem,
+        meta_send,
+        meta_recv,
+        move_send,
+        move_recv,
+        state_send,
+        state_recv,
+        far_send,
+        far_recv,
+        mid_send,
+        mid_recv,
+        near_send,
+        near_recv,
+        stat_send,
+        stat_recv,
+    ) = (refs[:5], refs[5:11]) + refs[11:]
     shards = moves_all.shape[0]
     me = lax.axis_index("seq")
     rows = pulled.shape[0]
@@ -296,8 +280,8 @@
     for i in range(tiles):
         fetch(i).start()
 
-    def send(source, target, send_sem, recv_sem, dest):
-        copy = pltpu.make_async_remote_copy(
+    def plan(source, target, send_sem, recv_sem, dest):
+        return pltpu.make_async_remote_copy(
             src_ref=source,
             dst_ref=target,
             send_sem=send_sem,
@@ -305,6 +289,9 @@
             device_id={"seq": dest},
             device_id_type=pl.DeviceIdType.MESH,
         )
+
+    def send(*route):
+        copy = plan(*route)
         copy.start()
         return copy
 
@@ -322,15 +309,54 @@
     arriving = []
     for k in range(1, shards):
         dest = lax.rem(me + k, shards)
-        small = send(meta, meta_all.at[me], meta_send.at[k], meta_recv.at[k], dest)
-        large = send(
-            moves.at[dest // copies], moves_all.at[me], move_send.at[k], move_recv.at[k], dest
-        )
-        arriving += [small, large]
+        arriving.append(
+            send(meta, meta_all.at[me], meta_send.at[k], meta_recv.at[k], dest)
+        )
     meta_all[me] = meta[...]
+
+    def move(unit, source, peer):
+        return plan(
+            moves.at[unit], moves_all.at[source], move_send.at[peer], move_recv.at[source], peer
+        )
+
+    diag_block = block_mask(WIDE, WIDE)
+    wide_ones = jnp.where(diag_block, 1.0, 0.0).astype(BF16)
+    per_group = WIDE // LANES
+
+    def state_step(i, carry):
+        for g in range(2):
+            s = pl.ds(pl.multiple_of((i * 2 + g) * WIDE, WIDE), WIDE)
+            passage, update, q, o = state_group(
+                [r[:, s] for r in prefix], [r[:, s] for r in answers], wide_ones, diag_block
+            )
+            pulled[:, s] = q
+            fresh[:, s] = o
+            for u in range(per_group):
+                lanes = slice(u * LANES, (u + 1) * LANES)
+                unit = (i * 2 + g) * per_group + u
+                moves[unit, :HSIZE] = passage[:, lanes]
+                moves[unit, HSIZE:] = update[:, lanes]
+        for u in range(2 * per_group):
+            unit = i * (2 * per_group) + u
+            for c in range(copies):
+                peer = unit * copies + c
+
+                @pl.when(peer != me)
+                def _():
+                    move(unit, me, peer).start()
+
+        return carry
+
+    lax.fori_loop(0, moves.shape[0] // (2 * per_group), state_step, 0)
     moves_all[me] = moves[me // copies]
     for copy in arriving:
         copy.wait_recv()
+    for source in range(shards):
+
+        @pl.when(source != me)
+        def _():
+            move(source // copies, source, source).wait_recv()
+
     sent += arriving
 
     docs = documents(lengths, moves_all)
@@ -447,6 +473,11 @@
         ).astype(F32)
     for copy in sent:
         copy.wait_send()
+    for peer in range(shards):
+
+        @pl.when(peer != me)
+        def _():
+            move(peer // copies, me, peer).wait_send()
 
 
 VMEM = pl.BlockSpec(memory_space=pltpu.VMEM)
@@ -463,26 +494,6 @@
     rows = answers[0].shape[0]
     units = width // LANES
     copies = max(shards // units, 1)
-    block = 2 * WIDE
-
-    moves, pulled, fresh = pl.pallas_call(
-        states_kernel,
-        grid=(width // block,),
-        in_specs=[pl.BlockSpec((tok_rows, block), lambda i: (0, i))] * 5
-        + [pl.BlockSpec((rows, block), lambda i: (0, i))] * 6,
-        out_specs=[
-            pl.BlockSpec((block // LANES, LANES, LANES), lambda i: (i, 0, 0)),
-            pl.BlockSpec((rows, block), lambda i: (0, i)),
-            pl.BlockSpec((rows, block), lambda i: (0, i)),
-        ],
-        out_shape=[
-            jax.ShapeDtypeStruct((units, LANES, LANES), F32),
-            jax.ShapeDtypeStruct((rows, width), F32),
-            jax.ShapeDtypeStruct((rows, width), F32),
-        ],
-        compiler_params=pltpu.CompilerParams(vmem_limit_bytes=60 * 2**20),
-        name="states",
-    )(*prefix, *answers)
     meta = jnp.concatenate(
         [choice_tokens.reshape(-1), jnp.broadcast_to(question_doc, (8,))]
     )
@@ -494,10 +505,13 @@
     dma = pltpu.SemaphoreType.DMA
     scores = pl.pallas_call(
         functools.partial(score_kernel, copies),
-        in_specs=[SMEM, SMEM, VMEM, VMEM, VMEM, VMEM, pl.BlockSpec(memory_space=pl.ANY)],
+        in_specs=[SMEM, SMEM] + [VMEM] * 12 + [pl.BlockSpec(memory_space=pl.ANY)],
         out_specs=VMEM,
         out_shape=jax.ShapeDtypeStruct((choices, LANES), F32),
         scratch_shapes=[
+            pltpu.VMEM((units, LANES, LANES), F32),
+            pltpu.VMEM((rows, width), F32),
+            pltpu.VMEM((rows, width), F32),
             pltpu.VMEM((shards, rows + 8, LANES), jnp.int32),
             pltpu.VMEM((shards, LANES, LANES), F32),
             pltpu.VMEM((shards, HSIZE, LANES), BF16),
@@ -516,7 +530,7 @@
             vmem_limit_bytes=60 * 2**20, collective_id=0, has_side_effects=True
         ),
         name="score",
-    )(doc_lengths, choice_lengths, meta, moves, pulled, fresh, head_weight)
+    )(doc_lengths, choice_lengths, meta, *prefix, *answers, head_weight)
     return scores[:, 0][None]
 
 

time: 136 us -> 120 us (0.88)
  Pallas kernels: 133 us -> 117 us
    pallas_call x1 -> x0, Pallas kernels: 37.6 us -> none  [local(): pl.pallas_call(states_kernel, grid=(width // block,), in_specs=[pl.BlockS...]
    pallas_call x1, Pallas kernels: 95.1 us -> 117 us  [local(): pl.pallas_call(functools.partial(score_kernel, copies), in_specs=[SMEM, S...]
where the time goes in v5:
time: 120 us
  Pallas kernels  117 us (98%)
  local copies, waits for them, and re-layouts  2.72 us (2%)
    pallas_call x1, Pallas kernels, local(): pl.pallas_call(functools.partial(score_kernel, copies), in_specs=[SMEM, S...  117 us

profile of v5, /device:TPU:0, one launch (start us, length us, event | category | flops | bytes accessed | tf_op | source)
XLA Modules:
  0.0 120.3 jit_solution(12844455067463967190)
XLA Ops:
  0.7 0.8 reshape.22
  1.4 0.7 broadcast_in_dim.5.meta
  2.1 116.9 %score.1 = f32[4,128]{1,0:T(4,128)} custom-call(s32[4]{0:T(128)} %lengths.1, s32[1,4]{1,0:T(1,128)} %choice_lengths.1, s32[40,128]{1,0:T(8,128)} %broadcast_in_dim.5.meta, bf16[128,2048]{1,0:T(8,128)(2,1)} %refs_0_.1, bf16[128,2048]{1,0:T(8,128)(2,1)} %refs_1_.1, bf16[128,2048]{1,0:T(8,128)(2,1)} %refs_2_.1, bf16[128,2048]{1,0:T(8,128)(2,1)} %refs_3_.1, ...), custom_call_target="tpu_custom_call" | custom-call | tf_op jit(solution)/shard_map/score/pallas_call | solution.py:506
  119.0 1.3 %slice_reduce_fusion = f32[4]{0:T(128)} fusion(f32[4,128]{1,0:T(4,128)} %score.1), kind=kLoop, calls=%fused_computation | loop fusion | bytes 32 | tf_op jit(solution)/shard_map/slice | solution.py:534
  (1 shorter events, 0.0 us)
